TPU v7x, 1024 devices: a whole 8x8x8 slice. The times are simulated.
1024 devices in a mesh: pipe: 16 (over z, x_lo), row: 8 (over x_hi, core), col: 8 (over y).
Axes of the slice: x: 8 (x_hi: 4, x_lo: 2; x = x_hi * 2 + x_lo), y: 8, z: 8, core: 2. Of those that a mesh axis runs over, the one named last changes fastest.
Arguments:
- weights: bfloat16 [16, 4096, 14336], P('pipe', 'col', 'row'), may hold values from -0.09375 to 0.09375
- fwd_resid: bfloat16 [16, 128, 4096], P('pipe', None, 'col'), may hold values from -6 to 6
- fwd_hidden: bfloat16 [16, 128, 14336], P('pipe', None, 'row'), may hold values from -6 to 6
- bwd_resid: bfloat16 [16, 128, 4096], P('pipe', None, 'col'), may hold values from -6 to 6
- bwd_hidden: bfloat16 [16, 128, 14336], P('pipe', None, 'row'), may hold values from -6 to 6
- saved_pre: bfloat16 [4, 16, 128, 14336], P(None, 'pipe', None, 'row'), may hold values from -6 to 6
- pool_embed: bfloat16 [3, 128, 4096], P(None, None, 'col'), may hold values from -6 to 6
- pool_mask: int32 [3, 128], replicated, may hold values 0 or 1
- pool_stratum: int32 [3], replicated, may hold values from 0 to 7
- order: int32 [3], replicated, may hold values from 0 to 2, each once
- mask_vec: bfloat16 [4096], P('col'), may hold values from -6 to 6
- ratio_table: bfloat16 [8, 4096], P(None, 'col'), may hold values from -6 to 6
- cot_inject: bfloat16 [3, 128, 4096], P(None, None, 'col'), may hold values from -6 to 6
Outputs:
- out_resid: bfloat16 [2, 16, 128, 4096], P(None, 'pipe', None, 'col')
- out_hidden: bfloat16 [16, 128, 14336], P('pipe', 'col', 'row')
Inputs may be any that keep to these rules, and one draw needn't show every extreme that they name: `order`: each waiting micro-batch enters exactly once.
All inputs are finite; a program needn't handle non-finite values.
Results may differ from a plain program's by a relative error of at most 0.025.
Values may be sent and summed in bfloat16 or wider, within the bound.
A program may use at most 64 MiB of HBM per device.

v0:
```python
import jax
import jax.numpy as jnp
from jax import lax
from jax.sharding import PartitionSpec as P

STEPS = 4


def cut_along(shard, dim, size):
    before, after = (shard.shape[:dim], shard.shape[dim + 1 :])
    return jnp.moveaxis(shard.reshape(*before, size, -1, *after), dim, 0)


def sent_and_summed(shard, axis, dim):
    tiles = cut_along(shard, dim, lax.axis_size(axis))
    arrived = lax.all_to_all(tiles, axis, split_axis=0, concat_axis=0, tiled=True)
    return arrived.astype(jnp.float32).sum(axis=0)


def from_everyone(shard, axis):
    size = lax.axis_size(axis)
    return lax.all_to_all(
        jnp.broadcast_to(shard[None], (size, *shard.shape)), axis, 0, 0, tiled=True
    )


def laid_out(tiles, dim):
    lengths = list(tiles.shape[1:])
    lengths[dim] *= tiles.shape[0]
    return jnp.moveaxis(tiles, 0, dim).reshape(lengths)


def gathered_copies(shard, axis, dim):
    tiles = from_everyone(shard, axis)
    return laid_out(tiles, dim)


def extended_2(shard, sides, width):
    for axis, dim in sides:
        size, length = (lax.axis_size(axis), shard.shape[dim])
        up = [(i, (i + 1) % size) for i in range(size - 1)]
        down = [(j, i) for i, j in up]
        last = lax.slice_in_dim(shard, length - width, length, axis=dim)
        first = lax.slice_in_dim(shard, 0, width, axis=dim)
        before = lax.ppermute(last, axis, up)
        after = lax.ppermute(first, axis, down)
        shard = jnp.concatenate([before, shard, after], axis=dim)
    return shard


def swapped(value, axis, stride):
    mask = 2**stride
    pairs = [(source, source ^ mask) for source in range(lax.axis_size(axis))]
    return lax.ppermute(value, axis, pairs)


def silu_grad(preact):
    sigma = jax.nn.sigmoid(preact)
    return sigma * (1.0 + preact * (1.0 - sigma))


def inject(step_idx, pool_embed, pool_mask, pool_stratum, order, mask_vec, ratio_table):
    chosen = order[step_idx - 1]
    embedded = pool_embed[chosen]
    masked = pool_mask[chosen]
    stratum = pool_stratum[chosen]
    onehot = (jnp.arange(ratio_table.shape[0], dtype=jnp.int32) == stratum).astype(jnp.bfloat16)
    condition = jnp.dot(onehot, ratio_table, preferred_element_type=jnp.float32)
    chosen_rows = jnp.where(
        masked[:, None] == 1, mask_vec[None, :].astype(jnp.float32), embedded.astype(jnp.float32)
    )
    return (chosen_rows + condition[None, :]).astype(jnp.bfloat16)


def shards(
    weights,
    fwd_resid,
    fwd_hidden,
    bwd_resid,
    bwd_hidden,
    saved_pre,
    pool_embed,
    pool_mask,
    pool_stratum,
    order,
    mask_vec,
    ratio_table,
    cot_inject,
):
    weight = weights[0]
    fwd_res = fwd_resid[0]
    fwd_hid = fwd_hidden[0]
    bwd_res = bwd_resid[0]
    bwd_hid = bwd_hidden[0]
    position = lax.axis_index("pipe")
    sections = lax.axis_size("pipe")
    is_even = position % 2 == 0
    token_rows = fwd_res.shape[0]
    col_rows = token_rows // lax.axis_size("col")
    fwd_out, bwd_out, hid_share = (fwd_res, bwd_res, fwd_hid)
    for step_idx in range(STEPS):
        operand = jnp.where(is_even, fwd_res, bwd_res)

        def feature_term(offset, length, operand=operand):
            return jnp.dot(operand, weight, preferred_element_type=jnp.float32)

        preact = sent_and_summed(
            feature_term(jnp.int32(0), col_rows * lax.axis_size("col")).astype(jnp.bfloat16),
            "col",
            0,
        )
        hid_share = jnp.where(is_even, jax.nn.silu(preact), preact).astype(jnp.bfloat16)
        hid_grad = (
            bwd_hid.astype(jnp.float32) * silu_grad(saved_pre[step_idx, 0].astype(jnp.float32))
        ).astype(jnp.bfloat16)
        hid_operand = jnp.where(is_even, hid_grad, fwd_hid)
        residual = jnp.where(is_even, bwd_res, fwd_res)
        row_rows = token_rows // lax.axis_size("row")

        def hidden_term(offset, length, hid_operand=hid_operand):
            return lax.dot_general(
                hid_operand, weight, (((1,), (1,)), ((), ())), preferred_element_type=jnp.float32
            )

        blended = sent_and_summed(
            hidden_term(jnp.int32(0), row_rows * lax.axis_size("row")).astype(jnp.bfloat16),
            "row",
            0,
        )
        res_share = lax.dynamic_slice_in_dim(
            residual, lax.axis_index("row") * row_rows, row_rows, 0
        )
        updated = gathered_copies(
            (res_share.astype(jnp.float32) + blended).astype(jnp.bfloat16), "row", 0
        )
        fwd_out = jnp.where(is_even, fwd_res, updated)
        bwd_out = jnp.where(is_even, updated, bwd_res)
        if step_idx + 1 < STEPS:
            res_rows = fwd_out.size // 128
            buffer = jnp.concatenate(
                [bwd_out.reshape(res_rows, 128), fwd_out.reshape(res_rows, 128)], 0
            )
            extended = extended_2(buffer, (("pipe", 0),), res_rows)
            left_resid = extended[:res_rows]
            right_resid = extended[extended.shape[0] - res_rows :]
            partner_hidden = swapped(hid_share, "pipe", 0)
            picked = jnp.where(is_even, partner_hidden, partner_hidden)
            gathered = gathered_copies(picked, "col", 0)
            fwd_hid = gathered
            bwd_hid = gathered
            incoming = inject(
                step_idx + 1, pool_embed, pool_mask, pool_stratum, order, mask_vec, ratio_table
            )
            fwd_res = jnp.where(position == 0, incoming, left_resid.reshape(fwd_out.shape))
            bwd_res = jnp.where(
                position == sections - 1, cot_inject[step_idx], right_resid.reshape(bwd_out.shape)
            )
    out_resid = jnp.stack([fwd_out, bwd_out])[:, None]
    return (out_resid, hid_share[None])


def solution(mesh):
    return jax.shard_map(
        shards,
        mesh=mesh,
        in_specs=(
            P("pipe", "col", "row"),
            P("pipe", None, "col"),
            P("pipe", None, "row"),
            P("pipe", None, "col"),
            P("pipe", None, "row"),
            P(None, "pipe", None, "row"),
            P(None, None, "col"),
            P(),
            P(),
            P(),
            P("col"),
            P(None, "col"),
            P(None, None, "col"),
        ),
        out_specs=(P(None, "pipe", None, "col"), P("pipe", "col", "row")),
        check_vma=False,
    )
```

profile of v0, /device:TPU:1, one launch (start us, length us, event | category | flops | bytes accessed | tf_op | source)
XLA Modules:
  0.0 295.3 jit_solution(3811000895062729774)
XLA Ops:
  0.7 1.5 copy-done
  2.1 2.6 fusion.12
  4.7 17.5 %all-to-all-start = ((bf16[8,16,512]{2,1,0:T(8,128)(2,1)}), bf16[8,16,512]{2,1,0:T(8,128)(2,1)S(1)}, u32[]{:S(2)}, u32[]{:S(2)}) async-start(bf16[8,16,512]{2,1,0:T(8,128)(2,1)} %bitcast.26), calls=%async_computation | async-start | bytes 262144 | tf_op jit(solution)/shard_map/all_to_all | solution.py:16
  22.3 1.2 convolution_convert_fusion.3
  23.5 6.8 %all-to-all-done = bf16[8,16,512]{2,1,0:T(8,128)(2,1)S(1)} async-done(((bf16[8,16,512]{2,1,0:T(8,128)(2,1)}), bf16[8,16,512]{2,1,0:T(8,128)(2,1)S(1)}, u32[]{:S(2)}, u32[]{:S(2)}) %all-to-all-start) | async-done | bytes 131104 | tf_op jit(solution)/shard_map/all_to_all | solution.py:16
  30.3 3.6 %all-to-all-start.2 = ((bf16[8,16,1792]{2,1,0:T(8,128)(2,1)}), bf16[8,16,1792]{2,1,0:T(8,128)(2,1)S(1)}, u32[]{:S(2)}, u32[]{:S(2)}) async-start(bf16[8,16,1792]{2,1,0:T(8,128)(2,1)} %bitcast.30), calls=%async_computation.2 | async-start | bytes 917504 | tf_op jit(solution)/shard_map/all_to_all | solution.py:16
  41.0 8.2 %all-to-all-done.2 = bf16[8,16,1792]{2,1,0:T(8,128)(2,1)S(1)} async-done(((bf16[8,16,1792]{2,1,0:T(8,128)(2,1)}), bf16[8,16,1792]{2,1,0:T(8,128)(2,1)S(1)}, u32[]{:S(2)}, u32[]{:S(2)}) %all-to-all-start.2) | async-done | bytes 458784 | tf_op jit(solution)/shard_map/all_to_all | solution.py:16
  49.9 4.9 %all-to-all-start.1 = ((bf16[8,16,512]{2,1,0:T(8,128)(2,1)}), bf16[8,16,512]{2,1,0:T(8,128)(2,1)S(1)}, u32[]{:S(2)}, u32[]{:S(2)}) async-start(bf16[8,16,512]{2,1,0:T(8,128)(2,1)} %broadcast_in_dim.123), calls=%async_computation.1 | async-start | bytes 262144 | tf_op jit(solution)/shard_map/all_to_all | solution.py:22
  54.9 1.9 collective-permute-start.2
  56.8 0.8 fusion.93
  57.6 5.3 %all-to-all-done.1 = bf16[8,16,512]{2,1,0:T(8,128)(2,1)S(1)} async-done(((bf16[8,16,512]{2,1,0:T(8,128)(2,1)}), bf16[8,16,512]{2,1,0:T(8,128)(2,1)S(1)}, u32[]{:S(2)}, u32[]{:S(2)}) %all-to-all-start.1) | async-done | bytes 131104 | tf_op jit(solution)/shard_map/all_to_all | solution.py:22
  62.9 0.8 broadcast_in_dim.126
  63.7 3.5 %all-to-all-start.3 = ((bf16[8,16,1792]{2,1,0:T(8,128)(2,1)}), bf16[8,16,1792]{2,1,0:T(8,128)(2,1)S(1)}, u32[]{:S(2)}, u32[]{:S(2)}) async-start(bf16[8,16,1792]{2,1,0:T(8,128)(2,1)} %broadcast_in_dim.126), calls=%async_computation.3 | async-start | bytes 917504 | tf_op jit(solution)/shard_map/all_to_all | solution.py:22
  70.0 2.5 dynamic-slice_convert_fusion.2
  72.5 0.9 fusion.111
  73.4 1.7 reshape.274
  75.0 7.5 %all-to-all-done.3 = bf16[8,16,1792]{2,1,0:T(8,128)(2,1)S(1)} async-done(((bf16[8,16,1792]{2,1,0:T(8,128)(2,1)}), bf16[8,16,1792]{2,1,0:T(8,128)(2,1)S(1)}, u32[]{:S(2)}, u32[]{:S(2)}) %all-to-all-start.3) | async-done | bytes 458784 | tf_op jit(solution)/shard_map/all_to_all | solution.py:22
  82.6 1.4 fusion.54
  84.0 1.4 fusion.15
  85.4 5.5 %all-to-all-start.4 = ((bf16[8,16,512]{2,1,0:T(8,128)(2,1)}), bf16[8,16,512]{2,1,0:T(8,128)(2,1)S(1)}, u32[]{:S(2)}, u32[]{:S(2)}) async-start(bf16[8,16,512]{2,1,0:T(8,128)(2,1)} %bitcast.34), calls=%async_computation.4 | async-start | bytes 262144 | tf_op jit(solution)/shard_map/all_to_all | solution.py:16
  90.9 1.6 broadcast_select_fusion.9
  92.5 1.3 collective-permute-start.1
  93.8 4.0 %collective-permute-start = (bf16[512,128]{1,0:T(8,128)(2,1)}, bf16[512,128]{1,0:T(8,128)(2,1)S(1)}, u32[]{:S(2)}, u32[]{:S(2)}) collective-permute-start(bf16[512,128]{1,0:T(8,128)(2,1)} %get-tuple-element.26), channel_id=1, source_target_pairs={{0,64},{64,128},{128,192},{192,256},{256,320},{320,384},{384,448},... | collective-permute-start | bytes 393224 | tf_op jit(solution)/shard_map/ppermute | solution.py:45
  97.8 1.3 fusion.113
  101.4 0.9 add_convert_fusion.6
  102.9 8.0 %all-to-all-start.5 = ((bf16[8,16,512]{2,1,0:T(8,128)(2,1)}), bf16[8,16,512]{2,1,0:T(8,128)(2,1)S(1)}, u32[]{:S(2)}, u32[]{:S(2)}) async-start(bf16[8,16,512]{2,1,0:T(8,128)(2,1)} %broadcast_in_dim.127), calls=%async_computation.5 | async-start | bytes 262144 | tf_op jit(solution)/shard_map/all_to_all | solution.py:22
  113.1 6.5 %all-to-all-done.5 = bf16[8,16,512]{2,1,0:T(8,128)(2,1)S(1)} async-done(((bf16[8,16,512]{2,1,0:T(8,128)(2,1)}), bf16[8,16,512]{2,1,0:T(8,128)(2,1)S(1)}, u32[]{:S(2)}, u32[]{:S(2)}) %all-to-all-start.5) | async-done | bytes 131104 | tf_op jit(solution)/shard_map/all_to_all | solution.py:22
  120.5 1.7 broadcast_select_fusion.5
  122.7 16.8 %all_to_all.75 = bf16[8,16,1792]{2,1,0:T(8,128)(2,1)S(1)} all-to-all(bf16[8,16,1792]{2,1,0:T(8,128)(2,1)S(1)} %bitcast.136), channel_id=1, replica_groups=mesh['pipe'=16,'row'=8,'col'=8] {'col'}, dimensions={0} | all-to-all | bytes 917504 | tf_op jit(solution)/shard_map/all_to_all | solution.py:16
  139.6 4.3 %collective-permute-start.5 = (bf16[16,1792]{1,0:T(8,128)(2,1)S(1)}, bf16[16,1792]{1,0:T(8,128)(2,1)S(1)}, u32[]{:S(2)}, u32[]{:S(2)}) collective-permute-start(bf16[16,1792]{1,0:T(8,128)(2,1)S(1)} %fusion.71), channel_id=1, source_target_pairs={{0,64},{64,0},{128,192},{192,128},{256,320},{320,256},{384,448},{4... | collective-permute-start | bytes 172040 | tf_op jit(solution)/shard_map/ppermute | solution.py:54
  144.0 1.6 collective-permute-done.5
  145.5 0.8 broadcast_in_dim.129
  146.3 3.5 %all-to-all-start.7 = ((bf16[8,16,1792]{2,1,0:T(8,128)(2,1)}), bf16[8,16,1792]{2,1,0:T(8,128)(2,1)S(1)}, u32[]{:S(2)}, u32[]{:S(2)}) async-start(bf16[8,16,1792]{2,1,0:T(8,128)(2,1)} %broadcast_in_dim.129), calls=%async_computation.7 | async-start | bytes 917504 | tf_op jit(solution)/shard_map/all_to_all | solution.py:22
  149.9 12.7 %all-to-all-done.7 = bf16[8,16,1792]{2,1,0:T(8,128)(2,1)S(1)} async-done(((bf16[8,16,1792]{2,1,0:T(8,128)(2,1)}), bf16[8,16,1792]{2,1,0:T(8,128)(2,1)S(1)}, u32[]{:S(2)}, u32[]{:S(2)}) %all-to-all-start.7) | async-done | bytes 458784 | tf_op jit(solution)/shard_map/all_to_all | solution.py:22
  163.0 1.4 fusion.18
  164.4 7.6 %all-to-all-start.8 = ((bf16[8,16,512]{2,1,0:T(8,128)(2,1)}), bf16[8,16,512]{2,1,0:T(8,128)(2,1)S(1)}, u32[]{:S(2)}, u32[]{:S(2)}) async-start(bf16[8,16,512]{2,1,0:T(8,128)(2,1)} %bitcast.41), calls=%async_computation.8 | async-start | bytes 262144 | tf_op jit(solution)/shard_map/all_to_all | solution.py:16
  172.0 3.4 %collective-permute-start.3 = (bf16[512,128]{1,0:T(8,128)(2,1)S(1)}, bf16[512,128]{1,0:T(8,128)(2,1)S(1)}, u32[]{:S(2)}, u32[]{:S(2)}) collective-permute-start(bf16[512,128]{1,0:T(8,128)(2,1)S(1)} %broadcast_select_fusion.7), channel_id=1, source_target_pairs={{0,64},{64,128},{128,192},{192,256},{256,320},{320,384},{384,448},... | collective-permute-start | bytes 393224 | tf_op jit(solution)/shard_map/ppermute | solution.py:45
  175.4 1.3 collective-permute-start.4
  177.4 2.3 collective-permute-done.3
  179.8 3.6 %collective-permute-done.4 = bf16[512,128]{1,0:T(8,128)(2,1)S(1)} collective-permute-done((bf16[512,128]{1,0:T(8,128)(2,1)}, bf16[512,128]{1,0:T(8,128)(2,1)S(1)}, u32[]{:S(2)}, u32[]{:S(2)}) %collective-permute-start.4) | collective-permute-done | bytes 131104 | tf_op jit(solution)/shard_map/ppermute | solution.py:46
  184.2 0.9 add_convert_fusion.5
  185.7 7.8 %all-to-all-start.9 = ((bf16[8,16,512]{2,1,0:T(8,128)(2,1)}), bf16[8,16,512]{2,1,0:T(8,128)(2,1)S(1)}, u32[]{:S(2)}, u32[]{:S(2)}) async-start(bf16[8,16,512]{2,1,0:T(8,128)(2,1)} %broadcast_in_dim.130), calls=%async_computation.9 | async-start | bytes 262144 | tf_op jit(solution)/shard_map/all_to_all | solution.py:22
  193.9 8.4 %all-to-all-done.9 = bf16[8,16,512]{2,1,0:T(8,128)(2,1)S(1)} async-done(((bf16[8,16,512]{2,1,0:T(8,128)(2,1)}), bf16[8,16,512]{2,1,0:T(8,128)(2,1)S(1)}, u32[]{:S(2)}, u32[]{:S(2)}) %all-to-all-start.9) | async-done | bytes 131104 | tf_op jit(solution)/shard_map/all_to_all | solution.py:22
  202.3 0.8 broadcast_select_fusion.4
  204.4 16.9 %all_to_all.76 = bf16[8,16,1792]{2,1,0:T(8,128)(2,1)S(1)} all-to-all(bf16[8,16,1792]{2,1,0:T(8,128)(2,1)S(1)} %bitcast.137), channel_id=1, replica_groups=mesh['pipe'=16,'row'=8,'col'=8] {'col'}, dimensions={0} | all-to-all | bytes 917504 | tf_op jit(solution)/shard_map/all_to_all | solution.py:16
  221.4 4.7 %collective-permute-start.8 = (bf16[16,1792]{1,0:T(8,128)(2,1)S(1)}, bf16[16,1792]{1,0:T(8,128)(2,1)S(1)}, u32[]{:S(2)}, u32[]{:S(2)}) collective-permute-start(bf16[16,1792]{1,0:T(8,128)(2,1)S(1)} %fusion.72), channel_id=1, source_target_pairs={{0,64},{64,0},{128,192},{192,128},{256,320},{320,256},{384,448},{4... | collective-permute-start | bytes 172040 | tf_op jit(solution)/shard_map/ppermute | solution.py:54
  226.2 1.6 collective-permute-done.8
  227.7 0.8 broadcast_in_dim.132
  228.5 3.5 %all-to-all-start.11 = ((bf16[8,16,1792]{2,1,0:T(8,128)(2,1)}), bf16[8,16,1792]{2,1,0:T(8,128)(2,1)S(1)}, u32[]{:S(2)}, u32[]{:S(2)}) async-start(bf16[8,16,1792]{2,1,0:T(8,128)(2,1)} %broadcast_in_dim.132), calls=%async_computation.11 | async-start | bytes 917504 | tf_op jit(solution)/shard_map/all_to_all | solution.py:22
  232.1 1.0 squeeze.65
  233.8 1.3 collective-permute-start.7
  235.1 4.0 %collective-permute-start.6 = (bf16[512,128]{1,0:T(8,128)(2,1)}, bf16[512,128]{1,0:T(8,128)(2,1)S(1)}, u32[]{:S(2)}, u32[]{:S(2)}) collective-permute-start(bf16[512,128]{1,0:T(8,128)(2,1)} %get-tuple-element.2), channel_id=1, source_target_pairs={{0,64},{64,128},{128,192},{192,256},{256,320},{320,384},{384,448},... | collective-permute-start | bytes 393224 | tf_op jit(solution)/shard_map/ppermute | solution.py:45
  240.0 1.3 collective-permute-done.6
  242.0 0.8 fusion.66
  242.9 1.2 convolution_convert_fusion
  244.8 5.8 %all-to-all-start.14 = ((bf16[8,16,1792]{2,1,0:T(8,128)(2,1)}), bf16[8,16,1792]{2,1,0:T(8,128)(2,1)S(1)}, u32[]{:S(2)}, u32[]{:S(2)}) async-start(bf16[8,16,1792]{2,1,0:T(8,128)(2,1)} %bitcast.53), calls=%async_computation.14 | async-start | bytes 917504 | tf_op jit(solution)/shard_map/all_to_all | solution.py:16
  251.1 1.4 fusion.21
  252.5 9.7 %all-to-all-done.14 = bf16[8,16,1792]{2,1,0:T(8,128)(2,1)S(1)} async-done(((bf16[8,16,1792]{2,1,0:T(8,128)(2,1)}), bf16[8,16,1792]{2,1,0:T(8,128)(2,1)S(1)}, u32[]{:S(2)}, u32[]{:S(2)}) %all-to-all-start.14) | async-done | bytes 458784 | tf_op jit(solution)/shard_map/all_to_all | solution.py:16
  262.2 9.0 %all-to-all-start.12 = ((bf16[8,16,512]{2,1,0:T(8,128)(2,1)}), bf16[8,16,512]{2,1,0:T(8,128)(2,1)S(1)}, u32[]{:S(2)}, u32[]{:S(2)}) async-start(bf16[8,16,512]{2,1,0:T(8,128)(2,1)} %bitcast.48), calls=%async_computation.12 | async-start | bytes 262144 | tf_op jit(solution)/shard_map/all_to_all | solution.py:16
  271.7 7.5 %all-to-all-done.12 = bf16[8,16,512]{2,1,0:T(8,128)(2,1)S(1)} async-done(((bf16[8,16,512]{2,1,0:T(8,128)(2,1)}), bf16[8,16,512]{2,1,0:T(8,128)(2,1)S(1)}, u32[]{:S(2)}, u32[]{:S(2)}) %all-to-all-start.12) | async-done | bytes 131104 | tf_op jit(solution)/shard_map/all_to_all | solution.py:16
  279.2 0.8 add_convert_fusion.4
  280.7 4.8 %all-to-all-start.13 = ((bf16[8,16,512]{2,1,0:T(8,128)(2,1)}), bf16[8,16,512]{2,1,0:T(8,128)(2,1)S(1)}, u32[]{:S(2)}, u32[]{:S(2)}) async-start(bf16[8,16,512]{2,1,0:T(8,128)(2,1)} %broadcast_in_dim.133), calls=%async_computation.13 | async-start | bytes 262144 | tf_op jit(solution)/shard_map/all_to_all | solution.py:22
  286.1 7.3 %all-to-all-done.13 = bf16[8,16,512]{2,1,0:T(8,128)(2,1)S(1)} async-done(((bf16[8,16,512]{2,1,0:T(8,128)(2,1)}), bf16[8,16,512]{2,1,0:T(8,128)(2,1)S(1)}, u32[]{:S(2)}, u32[]{:S(2)}) %all-to-all-start.13) | async-done | bytes 131104 | tf_op jit(solution)/shard_map/all_to_all | solution.py:22
  293.5 1.1 fusion.62
  (128 shorter events, 22.1 us)
Async XLA Ops:
  0.6 1.5 copy-start
  2.1 20.1 %copy-start.11 = (bf16[1,128,512]{2,1,0:T(8,128)(2,1)S(1)}, bf16[1,128,512]{2,1,0:T(8,128)(2,1)}, u32[]{:S(2)}) copy-start(bf16[1,128,512]{2,1,0:T(8,128)(2,1)} %param.14) | copy-start | bytes 393220
  2.1 20.1 %copy-start.12 = (bf16[1,128,512]{2,1,0:T(8,128)(2,1)S(1)}, bf16[1,128,512]{2,1,0:T(8,128)(2,1)}, u32[]{:S(2)}) copy-start(bf16[1,128,512]{2,1,0:T(8,128)(2,1)} %param.16) | copy-start | bytes 393220
  4.7 29.1 %copy-start.25 = (s32[3]{0:T(128)S(1)}, s32[3]{0:T(128)}, u32[]{:S(2)}) copy-start(s32[3]{0:T(128)} %param.22) | copy-start | bytes 40
  4.7 35.5 %copy-start.26 = (s32[3]{0:T(128)S(1)}, s32[3]{0:T(128)}, u32[]{:S(2)}) copy-start(s32[3]{0:T(128)} %param.21) | copy-start | bytes 40
  4.7 25.5 %all-to-all-start = ((bf16[8,16,512]{2,1,0:T(8,128)(2,1)}), bf16[8,16,512]{2,1,0:T(8,128)(2,1)S(1)}, u32[]{:S(2)}, u32[]{:S(2)}) async-start(bf16[8,16,512]{2,1,0:T(8,128)(2,1)} %bitcast.26), calls=%async_computation | async-start | bytes 262144 | tf_op jit(solution)/shard_map/all_to_all | solution.py:16
  22.3 34.6 %copy-start.22 = (bf16[8,512]{1,0:T(8,128)(2,1)S(1)}, bf16[8,512]{1,0:T(8,128)(2,1)}, u32[]{:S(2)}) copy-start(bf16[8,512]{1,0:T(8,128)(2,1)} %param.24) | copy-start | bytes 24580
  30.3 36.9 %copy-start.29 = (s32[3,128]{1,0:T(4,128)S(1)}, s32[3,128]{1,0:T(4,128)}, u32[]{:S(2)}) copy-start(s32[3,128]{1,0:T(4,128)} %param.20) | copy-start | bytes 4612
  30.3 18.9 %all-to-all-start.2 = ((bf16[8,16,1792]{2,1,0:T(8,128)(2,1)}), bf16[8,16,1792]{2,1,0:T(8,128)(2,1)S(1)}, u32[]{:S(2)}, u32[]{:S(2)}) async-start(bf16[8,16,1792]{2,1,0:T(8,128)(2,1)} %bitcast.30), calls=%async_computation.2 | async-start | bytes 917504 | tf_op jit(solution)/shard_map/all_to_all | solution.py:16
  33.9 36.1 %copy-start.10 = (bf16[3,128,512]{2,1,0:T(8,128)(2,1)S(1)}, bf16[3,128,512]{2,1,0:T(8,128)(2,1)}, u32[]{:S(2)}) copy-start(bf16[3,128,512]{2,1,0:T(8,128)(2,1)} %param.19) | copy-start | bytes 1179652
  49.9 13.0 %all-to-all-start.1 = ((bf16[8,16,512]{2,1,0:T(8,128)(2,1)}), bf16[8,16,512]{2,1,0:T(8,128)(2,1)S(1)}, u32[]{:S(2)}, u32[]{:S(2)}) async-start(bf16[8,16,512]{2,1,0:T(8,128)(2,1)} %broadcast_in_dim.123), calls=%async_computation.1 | async-start | bytes 262144 | tf_op jit(solution)/shard_map/all_to_all | solution.py:22
  54.9 8.0 %collective-permute-start.2 = (bf16[16,1792]{1,0:T(8,128)(2,1)S(1)}, bf16[16,1792]{1,0:T(8,128)(2,1)S(1)}, u32[]{:S(2)}, u32[]{:S(2)}) collective-permute-start(bf16[16,1792]{1,0:T(8,128)(2,1)S(1)} %fusion.70), channel_id=1, source_target_pairs={{0,64},{64,0},{128,192},{192,128},{256,320},{320,256},{384,448},{4... | collective-permute-start | bytes 172040 | tf_op jit(solution)/shard_map/ppermute | solution.py:54
  62.9 0.8 copy-start.15
  63.7 18.9 %all-to-all-start.3 = ((bf16[8,16,1792]{2,1,0:T(8,128)(2,1)}), bf16[8,16,1792]{2,1,0:T(8,128)(2,1)S(1)}, u32[]{:S(2)}, u32[]{:S(2)}) async-start(bf16[8,16,1792]{2,1,0:T(8,128)(2,1)} %broadcast_in_dim.126), calls=%async_computation.3 | async-start | bytes 917504 | tf_op jit(solution)/shard_map/all_to_all | solution.py:22
  67.8 4.7 %copy-start.28 = (pred[128]{0:T(512)(128)(4,1)}, pred[128]{0:T(512)(128)(4,1)S(1)}, u32[]{:S(2)}) copy-start(pred[128]{0:T(512)(128)(4,1)S(1)} %get-tuple-element.29) | copy-start | bytes 388
  70.0 2.5 copy-start.9
  84.0 6.9 %copy-start.16 = (bf16[512,128]{1,0:T(8,128)(2,1)S(1)}, bf16[512,128]{1,0:T(8,128)(2,1)}, u32[]{:S(2)}) copy-start(bf16[512,128]{1,0:T(8,128)(2,1)} %squeeze.57) | copy-start | bytes 393220
  84.0 6.9 %copy-start.17 = (bf16[512,128]{1,0:T(8,128)(2,1)S(1)}, bf16[512,128]{1,0:T(8,128)(2,1)}, u32[]{:S(2)}) copy-start(bf16[512,128]{1,0:T(8,128)(2,1)} %squeeze.60) | copy-start | bytes 393220
  85.4 25.5 %copy-start.14 = (bf16[1,128,512]{2,1,0:T(8,128)(2,1)S(1)}, bf16[1,128,512]{2,1,0:T(8,128)(2,1)}, u32[]{:S(2)}) copy-start(bf16[1,128,512]{2,1,0:T(8,128)(2,1)} %get-tuple-element.40) | copy-start | bytes 393220
  85.4 16.0 %all-to-all-start.4 = ((bf16[8,16,512]{2,1,0:T(8,128)(2,1)}), bf16[8,16,512]{2,1,0:T(8,128)(2,1)S(1)}, u32[]{:S(2)}, u32[]{:S(2)}) async-start(bf16[8,16,512]{2,1,0:T(8,128)(2,1)} %bitcast.34), calls=%async_computation.4 | async-start | bytes 262144 | tf_op jit(solution)/shard_map/all_to_all | solution.py:16
  92.5 6.9 %collective-permute-start.1 = (bf16[512,128]{1,0:T(8,128)(2,1)S(1)}, bf16[512,128]{1,0:T(8,128)(2,1)S(1)}, u32[]{:S(2)}, u32[]{:S(2)}) collective-permute-start(bf16[512,128]{1,0:T(8,128)(2,1)S(1)} %get-tuple-element.27), channel_id=1, source_target_pairs={{64,0},{128,64},{192,128},{256,192},{320,256},{384,320},{448,384},... | collective-permute-start | bytes 393224 | tf_op jit(solution)/shard_map/ppermute | solution.py:46
  93.8 6.9 %collective-permute-start = (bf16[512,128]{1,0:T(8,128)(2,1)}, bf16[512,128]{1,0:T(8,128)(2,1)S(1)}, u32[]{:S(2)}, u32[]{:S(2)}) collective-permute-start(bf16[512,128]{1,0:T(8,128)(2,1)} %get-tuple-element.26), channel_id=1, source_target_pairs={{0,64},{64,128},{128,192},{192,256},{256,320},{320,384},{384,448},... | collective-permute-start | bytes 393224 | tf_op jit(solution)/shard_map/ppermute | solution.py:45
  99.4 11.5 %copy-start.18 = (bf16[512,128]{1,0:T(8,128)(2,1)}, bf16[512,128]{1,0:T(8,128)(2,1)S(1)}, u32[]{:S(2)}) copy-start(bf16[512,128]{1,0:T(8,128)(2,1)S(1)} %collective-permute-done.1) | copy-start | bytes 393220
  100.6 2.3 copy-start.19
  102.9 16.7 %all-to-all-start.5 = ((bf16[8,16,512]{2,1,0:T(8,128)(2,1)}), bf16[8,16,512]{2,1,0:T(8,128)(2,1)S(1)}, u32[]{:S(2)}, u32[]{:S(2)}) async-start(bf16[8,16,512]{2,1,0:T(8,128)(2,1)} %broadcast_in_dim.127), calls=%async_computation.5 | async-start | bytes 262144 | tf_op jit(solution)/shard_map/all_to_all | solution.py:22
  119.7 3.0 %copy-start.5 = (bf16[512,128]{1,0:T(8,128)(2,1)}, bf16[512,128]{1,0:T(8,128)(2,1)S(1)}, u32[]{:S(2)}) copy-start(bf16[512,128]{1,0:T(8,128)(2,1)S(1)} %reshape.279) | copy-start | bytes 393220
  122.7 27.1 %copy-start.27 = (pred[128]{0:T(512)(128)(4,1)S(1)}, pred[128]{0:T(512)(128)(4,1)}, u32[]{:S(2)}) copy-start(pred[128]{0:T(512)(128)(4,1)} %get-tuple-element.30) | copy-start | bytes 388
  139.6 5.9 %collective-permute-start.5 = (bf16[16,1792]{1,0:T(8,128)(2,1)S(1)}, bf16[16,1792]{1,0:T(8,128)(2,1)S(1)}, u32[]{:S(2)}, u32[]{:S(2)}) collective-permute-start(bf16[16,1792]{1,0:T(8,128)(2,1)S(1)} %fusion.71), channel_id=1, source_target_pairs={{0,64},{64,0},{128,192},{192,128},{256,320},{320,256},{384,448},{4... | collective-permute-start | bytes 172040 | tf_op jit(solution)/shard_map/ppermute | solution.py:54
  146.3 16.3 %all-to-all-start.7 = ((bf16[8,16,1792]{2,1,0:T(8,128)(2,1)}), bf16[8,16,1792]{2,1,0:T(8,128)(2,1)S(1)}, u32[]{:S(2)}, u32[]{:S(2)}) async-start(bf16[8,16,1792]{2,1,0:T(8,128)(2,1)} %broadcast_in_dim.129), calls=%async_computation.7 | async-start | bytes 917504 | tf_op jit(solution)/shard_map/all_to_all | solution.py:22
  163.0 9.0 %copy-start.6 = (bf16[512,128]{1,0:T(8,128)(2,1)S(1)}, bf16[512,128]{1,0:T(8,128)(2,1)}, u32[]{:S(2)}) copy-start(bf16[512,128]{1,0:T(8,128)(2,1)} %copy-done.5) | copy-start | bytes 393220
  163.0 9.0 %copy-start.21 = (bf16[512,128]{1,0:T(8,128)(2,1)S(1)}, bf16[512,128]{1,0:T(8,128)(2,1)}, u32[]{:S(2)}) copy-start(bf16[512,128]{1,0:T(8,128)(2,1)} %get-tuple-element.5) | copy-start | bytes 393220
  163.0 30.5 %copy-start.8 = (f32[1,128,512]{2,1,0:T(8,128)S(1)}, f32[1,128,512]{2,1,0:T(8,128)}, u32[]{:S(2)}) copy-start(f32[1,128,512]{2,1,0:T(8,128)} %get-tuple-element.20) | copy-start | bytes 786436
  164.4 29.3 %copy-start.13 = (bf16[1,128,512]{2,1,0:T(8,128)(2,1)S(1)}, bf16[1,128,512]{2,1,0:T(8,128)(2,1)}, u32[]{:S(2)}) copy-start(bf16[1,128,512]{2,1,0:T(8,128)(2,1)} %get-tuple-element.39) | copy-start | bytes 393220
  164.4 19.7 %all-to-all-start.8 = ((bf16[8,16,512]{2,1,0:T(8,128)(2,1)}), bf16[8,16,512]{2,1,0:T(8,128)(2,1)S(1)}, u32[]{:S(2)}, u32[]{:S(2)}) async-start(bf16[8,16,512]{2,1,0:T(8,128)(2,1)} %bitcast.41), calls=%async_computation.8 | async-start | bytes 262144 | tf_op jit(solution)/shard_map/all_to_all | solution.py:16
  172.0 7.7 %collective-permute-start.3 = (bf16[512,128]{1,0:T(8,128)(2,1)S(1)}, bf16[512,128]{1,0:T(8,128)(2,1)S(1)}, u32[]{:S(2)}, u32[]{:S(2)}) collective-permute-start(bf16[512,128]{1,0:T(8,128)(2,1)S(1)} %broadcast_select_fusion.7), channel_id=1, source_target_pairs={{0,64},{64,128},{128,192},{192,256},{256,320},{320,384},{384,448},... | collective-permute-start | bytes 393224 | tf_op jit(solution)/shard_map/ppermute | solution.py:45
  175.4 8.0 %collective-permute-start.4 = (bf16[512,128]{1,0:T(8,128)(2,1)}, bf16[512,128]{1,0:T(8,128)(2,1)S(1)}, u32[]{:S(2)}, u32[]{:S(2)}) collective-permute-start(bf16[512,128]{1,0:T(8,128)(2,1)} %get-tuple-element.23), channel_id=1, source_target_pairs={{64,0},{128,64},{192,128},{256,192},{320,256},{384,320},{448,384},... | collective-permute-start | bytes 393224 | tf_op jit(solution)/shard_map/ppermute | solution.py:46
  179.7 13.8 %copy-start.20 = (bf16[512,128]{1,0:T(8,128)(2,1)}, bf16[512,128]{1,0:T(8,128)(2,1)S(1)}, u32[]{:S(2)}) copy-start(bf16[512,128]{1,0:T(8,128)(2,1)S(1)} %collective-permute-done.3) | copy-start | bytes 393220
  185.7 16.5 %all-to-all-start.9 = ((bf16[8,16,512]{2,1,0:T(8,128)(2,1)}), bf16[8,16,512]{2,1,0:T(8,128)(2,1)S(1)}, u32[]{:S(2)}, u32[]{:S(2)}) async-start(bf16[8,16,512]{2,1,0:T(8,128)(2,1)} %broadcast_in_dim.130), calls=%async_computation.9 | async-start | bytes 262144 | tf_op jit(solution)/shard_map/all_to_all | solution.py:22
  204.4 27.6 %copy-start.7 = (f32[1,128,512]{2,1,0:T(8,128)S(1)}, f32[1,128,512]{2,1,0:T(8,128)}, u32[]{:S(2)}) copy-start(f32[1,128,512]{2,1,0:T(8,128)} %get-tuple-element.15) | copy-start | bytes 786436
  204.4 28.7 %copy-start.23 = (pred[128]{0:T(512)(128)(4,1)S(1)}, pred[128]{0:T(512)(128)(4,1)}, u32[]{:S(2)}) copy-start(pred[128]{0:T(512)(128)(4,1)} %get-tuple-element.28) | copy-start | bytes 388
  221.4 6.3 %collective-permute-start.8 = (bf16[16,1792]{1,0:T(8,128)(2,1)S(1)}, bf16[16,1792]{1,0:T(8,128)(2,1)S(1)}, u32[]{:S(2)}, u32[]{:S(2)}) collective-permute-start(bf16[16,1792]{1,0:T(8,128)(2,1)S(1)} %fusion.72), channel_id=1, source_target_pairs={{0,64},{64,0},{128,192},{192,128},{256,320},{320,256},{384,448},{4... | collective-permute-start | bytes 172040 | tf_op jit(solution)/shard_map/ppermute | solution.py:54
  228.5 16.3 %all-to-all-start.11 = ((bf16[8,16,1792]{2,1,0:T(8,128)(2,1)}), bf16[8,16,1792]{2,1,0:T(8,128)(2,1)S(1)}, u32[]{:S(2)}, u32[]{:S(2)}) async-start(bf16[8,16,1792]{2,1,0:T(8,128)(2,1)} %broadcast_in_dim.132), calls=%async_computation.11 | async-start | bytes 917504 | tf_op jit(solution)/shard_map/all_to_all | solution.py:22
  233.8 6.2 %collective-permute-start.7 = (bf16[512,128]{1,0:T(8,128)(2,1)}, bf16[512,128]{1,0:T(8,128)(2,1)S(1)}, u32[]{:S(2)}, u32[]{:S(2)}) collective-permute-start(bf16[512,128]{1,0:T(8,128)(2,1)} %get-tuple-element.21), channel_id=1, source_target_pairs={{64,0},{128,64},{192,128},{256,192},{320,256},{384,320},{448,384},... | collective-permute-start | bytes 393224 | tf_op jit(solution)/shard_map/ppermute | solution.py:46
  235.1 6.2 %collective-permute-start.6 = (bf16[512,128]{1,0:T(8,128)(2,1)}, bf16[512,128]{1,0:T(8,128)(2,1)S(1)}, u32[]{:S(2)}, u32[]{:S(2)}) collective-permute-start(bf16[512,128]{1,0:T(8,128)(2,1)} %get-tuple-element.2), channel_id=1, source_target_pairs={{0,64},{64,128},{128,192},{192,256},{256,320},{320,384},{384,448},... | collective-permute-start | bytes 393224 | tf_op jit(solution)/shard_map/ppermute | solution.py:45
  240.0 1.4 copy-start.1
  241.3 0.7 copy-start.3
  244.8 17.3 %all-to-all-start.14 = ((bf16[8,16,1792]{2,1,0:T(8,128)(2,1)}), bf16[8,16,1792]{2,1,0:T(8,128)(2,1)S(1)}, u32[]{:S(2)}, u32[]{:S(2)}) async-start(bf16[8,16,1792]{2,1,0:T(8,128)(2,1)} %bitcast.53), calls=%async_computation.14 | async-start | bytes 917504 | tf_op jit(solution)/shard_map/all_to_all | solution.py:16
  250.7 20.5 %copy-start.24 = (pred[128]{0:T(512)(128)(4,1)S(1)}, pred[128]{0:T(512)(128)(4,1)}, u32[]{:S(2)}) copy-start(pred[128]{0:T(512)(128)(4,1)} %get-tuple-element.28) | copy-start | bytes 388
  250.7 20.6 %copy-start.2 = (bf16[512,128]{1,0:T(8,128)(2,1)S(1)}, bf16[512,128]{1,0:T(8,128)(2,1)}, u32[]{:S(2)}) copy-start(bf16[512,128]{1,0:T(8,128)(2,1)} %copy-done.1) | copy-start | bytes 393220
  250.7 20.6 %copy-start.4 = (bf16[512,128]{1,0:T(8,128)(2,1)S(1)}, bf16[512,128]{1,0:T(8,128)(2,1)}, u32[]{:S(2)}) copy-start(bf16[512,128]{1,0:T(8,128)(2,1)} %copy-done.3) | copy-start | bytes 393220
  262.2 17.0 %all-to-all-start.12 = ((bf16[8,16,512]{2,1,0:T(8,128)(2,1)}), bf16[8,16,512]{2,1,0:T(8,128)(2,1)S(1)}, u32[]{:S(2)}, u32[]{:S(2)}) async-start(bf16[8,16,512]{2,1,0:T(8,128)(2,1)} %bitcast.48), calls=%async_computation.12 | async-start | bytes 262144 | tf_op jit(solution)/shard_map/all_to_all | solution.py:16
  280.7 12.8 %all-to-all-start.13 = ((bf16[8,16,512]{2,1,0:T(8,128)(2,1)}), bf16[8,16,512]{2,1,0:T(8,128)(2,1)S(1)}, u32[]{:S(2)}, u32[]{:S(2)}) async-start(bf16[8,16,512]{2,1,0:T(8,128)(2,1)} %broadcast_in_dim.133), calls=%async_computation.13 | async-start | bytes 262144 | tf_op jit(solution)/shard_map/all_to_all | solution.py:22
where the time goes:
time: 299 us; the launch traced here: 295 us
  starting transfers between devices  111 us (37%)
  waiting for transfers between devices  92 us (31%)
  blocking collectives  33.7 us (11%)
  local copies, waits for them, and re-layouts  21.5 us (7%)
  other arithmetic  17.9 us (6%)
  matrix products  12.2 us (4%)
  between operations  7.03 us (2%)
    all_to_all x6, starting transfers between devices, sent_and_summed(): lax.all_to_all(tiles, axis, split_axis=0, concat_axis=0, tiled=True)  49 us
    all_to_all x7, waiting for transfers between devices, from_everyone(): lax.all_to_all(jnp.broadcast_to(shard[None], (size, *shard.shape)), axis,...  48.4 us
    all_to_all x7, starting transfers between devices, from_everyone(): lax.all_to_all(jnp.broadcast_to(shard[None], (size, *shard.shape)), axis,...  35.9 us
    all_to_all x2, blocking collectives, sent_and_summed(): lax.all_to_all(tiles, axis, split_axis=0, concat_axis=0, tiled=True)  33.7 us
    all_to_all x6, waiting for transfers between devices, sent_and_summed(): lax.all_to_all(tiles, axis, split_axis=0, concat_axis=0, tiled=True)  32.2 us
    ppermute x3, starting transfers between devices, extended_2(): before = lax.ppermute(last, axis, up)  11.4 us
    ppermute x3, starting transfers between devices, swapped(): return lax.ppermute(value, axis, pairs)  11 us
    dot_general x4, matrix products, hidden_term(): lax.dot_general(hid_operand, weight, (((1,), (1,)), ((), ())), preferred_...  6.72 us
  transfers between devices with their start and end apart: 22, of which 19 were waited for; matrix products, arithmetic and copies ran while one was open for 9% of the time, Pallas kernels for 0%

commit v1 on v0

v1 whole, which is shorter than its diff:
```python
import functools

import jax
import jax.numpy as jnp
from jax import lax
from jax.experimental import pallas as pl
from jax.experimental.pallas import tpu as pltpu
from jax.sharding import PartitionSpec as P

MESH = pl.DeviceIdType.MESH
STEPS = 4
F32 = jnp.float32
BF16 = jnp.bfloat16

FAR, IN_UP, IN_DN, NEAR_UP, NEAR_DN, SUM_UP, SUM_DN, SWAP = range(8)
GO_UP1, GO_DN1, GO_UP2, GO_DN2, FWD_UP, FWD_DN, FWD_FAR, RES = range(8, 16)
SPLIT = 16


def relay(
    sizes,
    weights,
    fwd_resid,
    fwd_hidden,
    bwd_resid,
    bwd_hidden,
    saved_pre,
    pool_embed,
    pool_mask,
    pool_stratum,
    order,
    mask_vec,
    ratio_table,
    cot_inject,
    out_resid,
    out_hidden,
    w,
    op,
    res0,
    hin,
    saved0,
    saved,
    embed,
    cot,
    part,
    far,
    inner,
    near,
    summed,
    total,
    hid,
    hid_in,
    blend,
    blend_in,
    res_in,
    upd,
    lsem,
    ssem,
    rsem,
):
    n_pipe, n_row, n_col = sizes
    p, r, c = lax.axis_index("pipe"), lax.axis_index("row"), lax.axis_index("col")
    odd = lax.rem(p, 2)
    even = odd == 0
    c_odd = lax.rem(c, 2)
    tc, tr = hid.shape[1], res_in.shape[1]
    tokens = tc * n_col
    n_hid, n_feat = w.shape[1], w.shape[0]

    def col_at(step):
        return lax.rem(c + (step + n_col), n_col)

    def row_at(step):
        return lax.rem(r + step, n_row)

    def pipe_at(step):
        return lax.rem(p + step + n_pipe, n_pipe)

    partner = p + 1 - 2 * odd
    facing = pipe_at(2 * odd - 1)
    onward = pipe_at(2 - 4 * odd)
    col_far = lax.rem(c + 2 + n_col - 4 * c_odd, n_col)

    barrier = pltpu.get_barrier_semaphore()
    greeted = [{"col": col_at(s)} for s in (1, -1, 2, -2)]
    greeted += [{"pipe": partner}, {"pipe": pipe_at(2)}, {"pipe": pipe_at(-2)}]
    greeted += [{"pipe": facing, "row": row_at(s)} for s in range(n_row)]
    greeted += [{"row": row_at(s)} for s in range(1, n_row)]
    for device in greeted:
        pl.semaphore_signal(barrier, inc=1, device_id=device, device_id_type=MESH)

    def load(slot, src, dst):
        return pltpu.make_async_copy(src, dst, lsem.at[slot])

    row_tile = pl.ds(pl.multiple_of(r * tr, tr), tr)
    col_tile = pl.ds(pl.multiple_of(c * tc, tc), tc)
    get_w = load(0, weights.at[0], w)
    get_op = load(1, fwd_resid.at[0], op.at[0])
    get_op_odd = load(1, bwd_resid.at[0], op.at[0])
    get_res = load(2, bwd_resid.at[0, row_tile], res0)
    get_res_odd = load(2, fwd_resid.at[0, row_tile], res0)
    get_hin = load(3, bwd_hidden.at[0], hin.at[0])
    get_hin_odd = load(3, fwd_hidden.at[0], hin.at[0])
    get_saved0 = load(4, saved_pre.at[0, 0], saved0)
    get_saved = load(5, saved_pre.at[pl.ds(1, STEPS - 1), 0, col_tile], saved)
    get_embed = load(6, pool_embed.at[:, row_tile], embed)
    get_cot = load(7, cot_inject.at[:, row_tile], cot)

    get_w.start()

    @pl.when(even)
    def _():
        get_op.start()
        get_hin.start()
        get_res.start()

    @pl.when(odd == 1)
    def _():
        get_op_odd.start()
        get_hin_odd.start()
        get_res_odd.start()

    get_saved0.start()
    get_saved.start()
    get_embed.start()
    get_cot.start()

    started = []

    def send(k, number, src, dst, device):
        copy = pltpu.make_async_remote_copy(
            src_ref=src,
            dst_ref=dst,
            send_sem=ssem.at[k, number],
            recv_sem=rsem.at[k, number],
            device_id=device,
            device_id_type=MESH,
        )
        copy.start()
        started.append(copy)
        return copy

    def col_view(x):
        return x.reshape(n_col, tc, x.shape[-1])

    def multiply_up(k):
        for at in range(0, n_hid, 256):
            cols = pl.ds(at, min(256, n_hid - at))
            out = jnp.dot(op[k], w[:, cols], preferred_element_type=F32)
            part[k, :, :, cols] = col_view(out.astype(BF16))

    def multiply_down(k):
        for at in range(0, n_feat, 256):
            cols = pl.ds(at, min(256, n_feat - at))
            out = lax.dot_general(
                hin[k], w[cols, :], (((1,), (1,)), ((), ())), preferred_element_type=F32
            )
            blend[k, :, :, cols] = out.astype(BF16).reshape(n_row, tr, -1)

    def hin_tile(k, t):
        return hin.at[k, pl.ds(pl.multiple_of(t * tc, tc), tc)]

    def sum_start(k):
        a = send(k, FAR, part.at[k, col_at(4)], far.at[k], {"col": col_far})
        b = send(k, IN_UP, part.at[k, col_at(3)], inner.at[k, 0], {"col": col_at(1)})
        d = send(k, IN_DN, part.at[k, col_at(-3)], inner.at[k, 1], {"col": col_at(-1)})
        e = send(k, NEAR_UP, part.at[k, col_at(1)], near.at[k, 0], {"col": col_at(1)})
        f = send(k, NEAR_DN, part.at[k, col_at(-1)], near.at[k, 1], {"col": col_at(-1)})
        return a, b, d, e, f

    def sum_middle(k, arriving):
        for copy in arriving[:3]:
            copy.wait_recv()
        from_far = far[k].astype(F32)
        up = part[k, col_at(2)].astype(F32) + inner[k, 0].astype(F32)
        summed[k, 0] = (up + jnp.where(c_odd == 0, from_far, 0.0)).astype(BF16)
        a = send(k, SUM_UP, summed.at[k, 0], total.at[k, 0], {"col": col_at(2)})
        down = part[k, col_at(-2)].astype(F32) + inner[k, 1].astype(F32)
        summed[k, 1] = (down + jnp.where(c_odd == 0, 0.0, from_far)).astype(BF16)
        b = send(k, SUM_DN, summed.at[k, 1], total.at[k, 1], {"col": col_at(-2)})
        return arriving[3], arriving[4], a, b

    def sum_end(k, arriving):
        for copy in arriving:
            copy.wait_recv()
        pre = part[k, c].astype(F32) + near[k, 0].astype(F32) + near[k, 1].astype(F32)
        pre = pre + total[k, 0].astype(F32) + total[k, 1].astype(F32)
        return jnp.where(even, pre / (1.0 + jnp.exp(-pre)), pre).astype(BF16)

    def swap_start(k, value):
        hid[k] = value
        return send(k, SWAP, hid.at[k], hid_in.at[k], {"pipe": partner})

    def slope(a):
        s = 1.0 / (1.0 + jnp.exp(-a))
        return s * (1.0 + a * (1.0 - s))

    def swap_end(k, arriving):
        arriving.wait_recv()
        gate = jnp.where(even, slope(saved[k].astype(F32)), 1.0)
        mine = hin_tile(k + 1, c)
        mine[...] = (hid_in[k].astype(F32) * gate).astype(BF16)
        return (
            send(k, GO_UP2, mine, mine, {"col": col_at(2)}),
            send(k, GO_DN2, mine, mine, {"col": col_at(-2)}),
            send(k, GO_UP1, mine, mine, {"col": col_at(1)}),
            send(k, GO_DN1, mine, mine, {"col": col_at(-1)}),
        )

    def forward(k, arriving):
        arriving[0].wait_recv()
        arriving[1].wait_recv()
        below, above = hin_tile(k + 1, col_at(-2)), hin_tile(k + 1, col_at(2))
        far_tile = hin_tile(k + 1, lax.rem(c + n_col - 2 + 4 * c_odd, n_col))
        return (
            send(k, FWD_FAR, far_tile, far_tile, {"col": col_far}),
            send(k, FWD_UP, below, below, {"col": col_at(1)}),
            send(k, FWD_DN, above, above, {"col": col_at(-1)}),
            arriving[2],
            arriving[3],
        )

    def blend_start(k):
        last = k == STEPS - 1
        copies = []
        if last:
            tile = op.at[k - 1, row_tile]
            copies.append(send(k, RES, tile, res_in.at[k], {"pipe": partner}))
        for s in range(1 if last else 0, n_row):
            row = row_at(s)
            device = {"row": row} if last else {"pipe": facing, "row": row}
            copies.append(send(k, SPLIT + s, blend.at[k, row], blend_in.at[k, s], device))
        return copies

    def blend_end(k, arriving):
        last = k == STEPS - 1
        for copy in arriving:
            copy.wait_recv()
        new = res_in[k].astype(F32)
        if last:
            new = new + blend[k, r].astype(F32)
        for s in range(1 if last else 0, n_row):
            new = new + blend_in[k, s].astype(F32)
        if not last:
            new = jnp.where(p == 0, injected(k), new)
            new = jnp.where(p == n_pipe - 1, cot[k].astype(F32), new)
        dst = upd if last else op.at[k + 1]
        mine = dst.at[row_tile]
        mine[...] = new.astype(BF16)
        return [
            send(k, SPLIT + n_row + s, mine, mine, {"row": row_at(s)}) for s in range(1, n_row)
        ]

    def pick(index, ref):
        value = ref[ref.shape[0] - 1]
        for i in range(ref.shape[0] - 1):
            value = jnp.where(index == i, ref[i], value)
        return value

    def injected(k):
        chosen = order[k]
        stratum = pick(chosen, pool_stratum)
        mask = pool_mask[pl.ds(pool_mask.shape[0] - 1, 1), :]
        for i in range(pool_mask.shape[0] - 1):
            mask = jnp.where(chosen == i, pool_mask[pl.ds(i, 1), :], mask)
        here = lax.broadcasted_iota(jnp.int32, (tr, tokens), 0) + r * tr
        there = lax.broadcasted_iota(jnp.int32, (tr, tokens), 1)
        column = jnp.where(here == there, jnp.broadcast_to(mask, (tr, tokens)), 0)
        masked = jnp.sum(column.astype(F32), axis=1, keepdims=True) == 1.0
        table = ratio_table[...].astype(F32)
        strata = lax.broadcasted_iota(jnp.int32, table.shape, 0)
        condition = jnp.sum(jnp.where(strata == stratum, table, 0.0), axis=0, keepdims=True)
        vec = jnp.broadcast_to(mask_vec[...].astype(F32), (tr, n_feat))
        rows = jnp.where(masked, vec, pick(chosen, embed).astype(F32))
        return rows + condition

    def wait_all(copies):
        for copy in copies:
            copy.wait_recv()

    get_op.wait()
    get_w.wait()
    multiply_up(0)
    pl.semaphore_wait(barrier, len(greeted))
    x = sum_start(0)

    get_hin.wait()
    get_saved0.wait()
    gate = jnp.where(even, slope(saved0[...].astype(F32)), 1.0)
    hin[0] = (hin[0].astype(F32) * gate).astype(BF16)
    multiply_down(0)
    get_res.wait()
    y = blend_start(0)
    y.append(send(0, RES, res0, res_in.at[0], {"pipe": facing}))
    get_saved.wait()
    get_embed.wait()
    get_cot.wait()

    def send_res(k):
        tile = op.at[k, row_tile]
        return send(k + 1, RES, tile, res_in.at[k + 1], {"pipe": onward})

    res = send_res(0)
    x = sum_middle(0, x)
    y = blend_end(0, y)
    x = swap_start(0, sum_end(0, x))
    x = swap_end(0, x)
    wait_all(y)
    multiply_up(1)
    y = sum_start(1)
    next_res = send_res(1)
    x = forward(0, x)
    y = sum_middle(1, y)
    wait_all(x)
    multiply_down(1)
    x = blend_start(1) + [res]
    y = swap_start(1, sum_end(1, y))
    y = swap_end(1, y)
    x = blend_end(1, x)
    y = forward(1, y)
    wait_all(x)
    multiply_up(2)
    x = sum_start(2)
    wait_all(y)
    multiply_down(2)
    y = blend_start(2) + [next_res]
    x = sum_middle(2, x)
    y = blend_end(2, y)
    x = swap_start(2, sum_end(2, x))
    x = swap_end(2, x)
    wait_all(y)
    multiply_up(3)
    y = sum_start(3)
    out_resid[odd, 0] = op[3]
    x = forward(2, x)
    y = sum_middle(3, y)
    wait_all(x)
    multiply_down(3)
    x = blend_start(3)
    out_hidden[0] = sum_end(3, y)
    x = blend_end(3, x)
    wait_all(x)
    out_resid[1 - odd, 0] = upd[...]
    for copy in started:
        copy.wait_send()


def solution(mesh):
    sizes = tuple(mesh.shape[a] for a in ("pipe", "row", "col"))
    n_pipe, n_row, n_col = sizes

    def shards(weights, fwd_resid, fwd_hidden, *rest):
        _, tokens, n_feat = fwd_resid.shape
        n_hid = fwd_hidden.shape[2]
        tc, tr = tokens // n_col, tokens // n_row
        pool = rest[3].shape[0]
        args = [weights, fwd_resid, fwd_hidden, *rest]
        args[10] = args[10].reshape(1, n_feat)
        hbm = pl.BlockSpec(memory_space=pl.ANY)
        vmem = pl.BlockSpec(memory_space=pltpu.VMEM)
        smem = pl.BlockSpec(memory_space=pltpu.SMEM)
        in_specs = [hbm] * 7 + [vmem, smem, smem, vmem, vmem, hbm]
        copies = SPLIT + 2 * n_row
        return pl.pallas_call(
            functools.partial(relay, sizes),
            out_shape=(
                jax.ShapeDtypeStruct((2, 1, tokens, n_feat), BF16),
                jax.ShapeDtypeStruct((1, tc, n_hid), BF16),
            ),
            in_specs=in_specs,
            out_specs=(vmem, vmem),
            scratch_shapes=[
                pltpu.VMEM((n_feat, n_hid), BF16),
                pltpu.VMEM((STEPS, tokens, n_feat), BF16),
                pltpu.VMEM((tr, n_feat), BF16),
                pltpu.VMEM((STEPS, tokens, n_hid), BF16),
                pltpu.VMEM((tokens, n_hid), BF16),
                pltpu.VMEM((STEPS - 1, tc, n_hid), BF16),
                pltpu.VMEM((pool, tr, n_feat), BF16),
                pltpu.VMEM((pool, tr, n_feat), BF16),
                pltpu.VMEM((STEPS, n_col, tc, n_hid), BF16),
                pltpu.VMEM((STEPS, tc, n_hid), BF16),
                pltpu.VMEM((STEPS, 2, tc, n_hid), BF16),
                pltpu.VMEM((STEPS, 2, tc, n_hid), BF16),
                pltpu.VMEM((STEPS, 2, tc, n_hid), BF16),
                pltpu.VMEM((STEPS, 2, tc, n_hid), BF16),
                pltpu.VMEM((STEPS, tc, n_hid), BF16),
                pltpu.VMEM((STEPS, tc, n_hid), BF16),
                pltpu.VMEM((STEPS, n_row, tr, n_feat), BF16),
                pltpu.VMEM((STEPS, n_row, tr, n_feat), BF16),
                pltpu.VMEM((STEPS, tr, n_feat), BF16),
                pltpu.VMEM((tokens, n_feat), BF16),
                pltpu.SemaphoreType.DMA((8,)),
                pltpu.SemaphoreType.DMA((STEPS, copies)),
                pltpu.SemaphoreType.DMA((STEPS, copies)),
            ],
            compiler_params=pltpu.CompilerParams(
                collective_id=0, has_side_effects=True, vmem_limit_bytes=48 * 2**20
            ),
        )(*args)

    return jax.shard_map(
        shards,
        mesh=mesh,
        in_specs=(
            P("pipe", "col", "row"),
            P("pipe", None, "col"),
            P("pipe", None, "row"),
            P("pipe", None, "col"),
            P("pipe", None, "row"),
            P(None, "pipe", None, "row"),
            P(None, None, "col"),
            P(),
            P(),
            P(),
            P("col"),
            P(None, "col"),
            P(None, None, "col"),
        ),
        out_specs=(P(None, "pipe", None, "col"), P("pipe", "col", "row")),
        check_vma=False,
    )
```

time: 299 us -> 119 us (0.40); the launches traced: 295 us -> 118 us
  starting transfers between devices: 111 us -> 0 us
  Pallas kernels: 0 us -> 104 us
  waiting for transfers between devices: 92 us -> 0 us
  blocking collectives: 33.7 us -> 0 us
  other arithmetic: 17.9 us -> 0 us
  matrix products: 12.2 us -> 0 us
  local copies, waits for them, and re-layouts: 21.5 us -> 13.5 us
  between operations: 7.03 us -> 0.65 us
    pallas_call x0 -> x1, Pallas kernels: none -> 104 us  [shards(): pl.pallas_call(functools.partial(relay, sizes), out_shape=(jax.ShapeDtype...]
    all_to_all x13 -> x0, starting transfers between devices: 84.9 us -> none  [the longest x6 49 us: sent_and_summed(): lax.all_to_all(tiles, axis, split_axis=0, concat_axis=0, tiled=True)]
    all_to_all x13 -> x0, waiting for transfers between devices: 80.6 us -> none  [the longest x7 48.4 us: from_everyone(): lax.all_to_all(jnp.broadcast_to(shard[None], (size, *shard.shape)), axis,...]
    all_to_all x2 -> x0, blocking collectives: 33.7 us -> none  [sent_and_summed(): lax.all_to_all(tiles, axis, split_axis=0, concat_axis=0, tiled=True)]
    ppermute x9 -> x0, starting transfers between devices: 26.2 us -> none  [the longest x3 11.4 us: extended_2(): before = lax.ppermute(last, axis, up)]
    dot_general x11 -> x0, matrix products: 12.2 us -> none  [the longest x4 6.72 us: hidden_term(): lax.dot_general(hid_operand, weight, (((1,), (1,)), ((), ())), preferred_...]
    ppermute x9 -> x0, waiting for transfers between devices: 11.4 us -> none  [the longest x3 4.13 us: extended_2(): before = lax.ppermute(last, axis, up)]
    unnamed x60 -> x26, local copies, waits for them, and re-layouts: 2.21 us -> 12.8 us
  transfers between devices with their start and end apart: 22 -> 0, of which waited for: 19 -> 0; matrix products, arithmetic and copies ran while one was open for 9% -> 0% of each run, Pallas kernels for 0% -> 0%
where the time goes in v1:
time: 119 us; the launch traced here: 118 us
  Pallas kernels  104 us (87%)
  local copies, waits for them, and re-layouts  13.5 us (11%)
    pallas_call x1, Pallas kernels, shards(): pl.pallas_call(functools.partial(relay, sizes), out_shape=(jax.ShapeDtype...  104 us
    unnamed x26, local copies, waits for them, and re-layouts  12.8 us

profile of v1, /device:TPU:1, one launch (start us, length us, event | category | flops | bytes accessed | tf_op | source)
XLA Modules:
  0.0 118.3 jit_solution(14545422108116248273)
XLA Ops:
  0.6 0.7 reshape.7.mask_vec
  1.3 0.0 copy-start
  1.3 1.5 %copy-done = bf16[1,512,1792]{2,1,0:T(8,128)(2,1)S(1)} copy-done((bf16[1,512,1792]{2,1,0:T(8,128)(2,1)S(1)}, bf16[1,512,1792]{2,1,0:T(8,128)(2,1)}, u32[]{:S(2)}) %copy-start) | copy-done | bytes 1835032
  2.8 0.0 copy-start.1
  2.8 1.5 %copy-done.1 = bf16[4,1,128,1792]{3,2,1,0:T(8,128)(2,1)S(1)} copy-done((bf16[4,1,128,1792]{3,2,1,0:T(8,128)(2,1)S(1)}, bf16[4,1,128,1792]{3,2,1,0:T(8,128)(2,1)}, u32[]{:S(2)}) %copy-start.1) | copy-done | bytes 1835032
  4.3 0.0 copy-start.2
  4.3 1.0 copy-done.2
  5.3 0.0 copy-start.3
  5.3 1.0 copy-done.3
  6.4 0.0 copy-start.4
  6.4 1.0 copy-done.4
  7.3 0.0 copy-start.5
  7.3 1.0 copy-done.5
  8.3 0.0 copy-start.6
  8.3 0.9 copy-done.6
  9.2 0.0 copy-start.7
  9.2 0.9 copy-done.7
  10.2 0.0 copy-start.8
  10.2 0.7 copy-done.8
  10.8 0.0 copy-start.9
  10.9 0.7 copy-done.9
  11.5 0.0 copy-start.10
  11.5 0.7 copy-done.10
  12.2 0.0 copy-start.11
  12.2 0.7 copy-done.11
  12.8 104.2 %shard_map.140 = (bf16[2,1,128,512]{3,2,1,0:T(8,128)(2,1)S(1)}, bf16[1,16,1792]{2,1,0:T(8,128)(2,1)S(1)}) custom-call(bf16[1,512,1792]{2,1,0:T(8,128)(2,1)S(1)} %copy-done, bf16[1,128,512]{2,1,0:T(8,128)(2,1)S(1)} %copy-done.6, bf16[1,128,1792]{2,1,0:T(8,128)(2,1)S(1)} %copy-done.2, bf16[1,128,512]{2,1,0:T(8,128)(2,1)S(1)} %copy-done.7, ...), custom_call_target="tpu_custom_call" | custom-call | tf_op jit(solution)/shard_map/pallas_call | solution.py:364
  117.0 0.7 copy.17
  117.7 0.6 copy.18
Async XLA Ops:
  1.3 1.5 %copy-start = (bf16[1,512,1792]{2,1,0:T(8,128)(2,1)S(1)}, bf16[1,512,1792]{2,1,0:T(8,128)(2,1)}, u32[]{:S(2)}) copy-start(bf16[1,512,1792]{2,1,0:T(8,128)(2,1)} %weights.1) | copy-start | bytes 5505028
  2.8 1.5 %copy-start.1 = (bf16[4,1,128,1792]{3,2,1,0:T(8,128)(2,1)S(1)}, bf16[4,1,128,1792]{3,2,1,0:T(8,128)(2,1)}, u32[]{:S(2)}) copy-start(bf16[4,1,128,1792]{3,2,1,0:T(8,128)(2,1)} %saved_pre.1) | copy-start | bytes 5505028
  4.3 1.0 copy-start.2
  5.3 1.0 copy-start.3
  6.4 1.0 copy-start.4
  7.3 1.0 copy-start.5
  8.3 0.9 copy-start.6
  9.2 0.9 copy-start.7
  10.2 0.7 copy-start.8
  10.8 0.7 copy-start.9
  11.5 0.7 copy-start.10
  12.2 0.7 copy-start.11

commit v2 on v1

--- a/solution.py
+++ b/solution.py
@@ -42,6 +42,11 @@
     saved,
     embed,
     cot,
+    mask_in,
+    stratum_in,
+    order_in,
+    vec_in,
+    table_in,
     part,
     far,
     inner,
@@ -103,8 +108,6 @@
     get_hin_odd = load(3, fwd_hidden.at[0], hin.at[0])
     get_saved0 = load(4, saved_pre.at[0, 0], saved0)
     get_saved = load(5, saved_pre.at[pl.ds(1, STEPS - 1), 0, col_tile], saved)
-    get_embed = load(6, pool_embed.at[:, row_tile], embed)
-    get_cot = load(7, cot_inject.at[:, row_tile], cot)
 
     get_w.start()
 
@@ -112,6 +115,7 @@
     def _():
         get_op.start()
         get_hin.start()
+        get_saved0.start()
         get_res.start()
 
     @pl.when(odd == 1)
@@ -120,10 +124,18 @@
         get_hin_odd.start()
         get_res_odd.start()
 
-    get_saved0.start()
     get_saved.start()
-    get_embed.start()
-    get_cot.start()
+    small = [
+        load(6, pool_embed.at[:, row_tile], embed),
+        load(7, cot_inject.at[:, row_tile], cot),
+        load(8, pool_mask, mask_in),
+        load(9, pool_stratum, stratum_in),
+        load(10, order, order_in),
+        load(11, mask_vec, vec_in),
+        load(12, ratio_table, table_in),
+    ]
+    for copy in small:
+        copy.start()
 
     started = []
 
@@ -258,19 +270,19 @@
         return value
 
     def injected(k):
-        chosen = order[k]
-        stratum = pick(chosen, pool_stratum)
-        mask = pool_mask[pl.ds(pool_mask.shape[0] - 1, 1), :]
-        for i in range(pool_mask.shape[0] - 1):
-            mask = jnp.where(chosen == i, pool_mask[pl.ds(i, 1), :], mask)
+        chosen = order_in[k]
+        stratum = pick(chosen, stratum_in)
+        mask = mask_in[pl.ds(mask_in.shape[0] - 1, 1), :]
+        for i in range(mask_in.shape[0] - 1):
+            mask = jnp.where(chosen == i, mask_in[pl.ds(i, 1), :], mask)
         here = lax.broadcasted_iota(jnp.int32, (tr, tokens), 0) + r * tr
         there = lax.broadcasted_iota(jnp.int32, (tr, tokens), 1)
         column = jnp.where(here == there, jnp.broadcast_to(mask, (tr, tokens)), 0)
         masked = jnp.sum(column.astype(F32), axis=1, keepdims=True) == 1.0
-        table = ratio_table[...].astype(F32)
+        table = table_in[...].astype(F32)
         strata = lax.broadcasted_iota(jnp.int32, table.shape, 0)
         condition = jnp.sum(jnp.where(strata == stratum, table, 0.0), axis=0, keepdims=True)
-        vec = jnp.broadcast_to(mask_vec[...].astype(F32), (tr, n_feat))
+        vec = jnp.broadcast_to(vec_in[...].astype(F32)[None], (tr, n_feat))
         rows = jnp.where(masked, vec, pick(chosen, embed).astype(F32))
         return rows + condition
 
@@ -285,16 +297,19 @@
     x = sum_start(0)
 
     get_hin.wait()
-    get_saved0.wait()
-    gate = jnp.where(even, slope(saved0[...].astype(F32)), 1.0)
-    hin[0] = (hin[0].astype(F32) * gate).astype(BF16)
+
+    @pl.when(even)
+    def _():
+        get_saved0.wait()
+        hin[0] = (hin[0].astype(F32) * slope(saved0[...].astype(F32))).astype(BF16)
+
     multiply_down(0)
     get_res.wait()
     y = blend_start(0)
     y.append(send(0, RES, res0, res_in.at[0], {"pipe": facing}))
     get_saved.wait()
-    get_embed.wait()
-    get_cot.wait()
+    for copy in small:
+        copy.wait()
 
     def send_res(k):
         tile = op.at[k, row_tile]
@@ -354,12 +369,8 @@
         n_hid = fwd_hidden.shape[2]
         tc, tr = tokens // n_col, tokens // n_row
         pool = rest[3].shape[0]
-        args = [weights, fwd_resid, fwd_hidden, *rest]
-        args[10] = args[10].reshape(1, n_feat)
         hbm = pl.BlockSpec(memory_space=pl.ANY)
         vmem = pl.BlockSpec(memory_space=pltpu.VMEM)
-        smem = pl.BlockSpec(memory_space=pltpu.SMEM)
-        in_specs = [hbm] * 7 + [vmem, smem, smem, vmem, vmem, hbm]
         copies = SPLIT + 2 * n_row
         return pl.pallas_call(
             functools.partial(relay, sizes),
@@ -367,7 +378,7 @@
                 jax.ShapeDtypeStruct((2, 1, tokens, n_feat), BF16),
                 jax.ShapeDtypeStruct((1, tc, n_hid), BF16),
             ),
-            in_specs=in_specs,
+            in_specs=[hbm] * 13,
             out_specs=(vmem, vmem),
             scratch_shapes=[
                 pltpu.VMEM((n_feat, n_hid), BF16),
@@ -378,6 +389,11 @@
                 pltpu.VMEM((STEPS - 1, tc, n_hid), BF16),
                 pltpu.VMEM((pool, tr, n_feat), BF16),
                 pltpu.VMEM((pool, tr, n_feat), BF16),
+                pltpu.VMEM((pool, tokens), jnp.int32),
+                pltpu.SMEM((pool,), jnp.int32),
+                pltpu.SMEM((pool,), jnp.int32),
+                pltpu.VMEM((n_feat,), BF16),
+                pltpu.VMEM((rest[8].shape[0], n_feat), BF16),
                 pltpu.VMEM((STEPS, n_col, tc, n_hid), BF16),
                 pltpu.VMEM((STEPS, tc, n_hid), BF16),
                 pltpu.VMEM((STEPS, 2, tc, n_hid), BF16),
@@ -390,14 +406,14 @@
                 pltpu.VMEM((STEPS, n_row, tr, n_feat), BF16),
                 pltpu.VMEM((STEPS, tr, n_feat), BF16),
                 pltpu.VMEM((tokens, n_feat), BF16),
-                pltpu.SemaphoreType.DMA((8,)),
+                pltpu.SemaphoreType.DMA((13,)),
                 pltpu.SemaphoreType.DMA((STEPS, copies)),
                 pltpu.SemaphoreType.DMA((STEPS, copies)),
             ],
             compiler_params=pltpu.CompilerParams(
-                collective_id=0, has_side_effects=True, vmem_limit_bytes=48 * 2**20
+                collective_id=0, has_side_effects=True, vmem_limit_bytes=60 * 1024 * 1024
             ),
-        )(*args)
+        )(weights, fwd_resid, fwd_hidden, *rest)
 
     return jax.shard_map(
         shards,

time: 119 us -> 109 us (0.916)
  local copies, waits for them, and re-layouts: 13.5 us -> 3.11 us
    unnamed x26 -> x2, local copies, waits for them, and re-layouts: 12.8 us -> 3.11 us
where the time goes in v2:
time: 109 us; the launch traced here: 108 us
  Pallas kernels  104 us (95%)
  local copies, waits for them, and re-layouts  3.11 us (3%)
    pallas_call x1, Pallas kernels, shards(): pl.pallas_call(functools.partial(relay, sizes), out_shape=(jax.ShapeDtype...  104 us
    unnamed x2, local copies, waits for them, and re-layouts  3.11 us

profile of v2, /device:TPU:1, one launch (start us, length us, event | category | flops | bytes accessed | tf_op | source)
XLA Modules:
  0.0 107.7 jit_solution(3970144077055012977)
XLA Ops:
  0.6 104.0 %shard_map.140 = (bf16[2,1,128,512]{3,2,1,0:T(8,128)(2,1)}, bf16[1,16,1792]{2,1,0:T(8,128)(2,1)}) custom-call(bf16[1,512,1792]{2,1,0:T(8,128)(2,1)} %weights.1, bf16[1,128,512]{2,1,0:T(8,128)(2,1)} %fwd_resid.1, bf16[1,128,1792]{2,1,0:T(8,128)(2,1)} %fwd_hidden.1, bf16[1,128,512]{2,1,0:T(8,128)(2,1)} %bwd_resid.1, bf16[1,128,1792]{2,1,0:T(8,128)(2,1)} %bwd_hidden.1, ...), custom_call_target="tpu_custom_call" | custom-call | tf_op jit(solution)/shard_map/pallas_call | solution.py:375
  104.6 1.7 %copy.17 = bf16[2,1,128,512]{3,2,1,0:T(8,128)(2,1)} copy(bf16[2,1,128,512]{3,2,1,0:T(8,128)(2,1)} %get-tuple-element.4) | data formatting | bytes 524288
  106.3 1.4 %copy.18 = bf16[1,16,1792]{2,1,0:T(8,128)(2,1)} copy(bf16[1,16,1792]{2,1,0:T(8,128)(2,1)} %get-tuple-element.5) | data formatting | bytes 114688

commit v3 on v2

v3 whole, which is shorter than its diff:
```python
import functools

import jax
import jax.numpy as jnp
from jax import lax
from jax.experimental import pallas as pl
from jax.experimental.pallas import tpu as pltpu
from jax.sharding import PartitionSpec as P

MESH = pl.DeviceIdType.MESH
STEPS = 4
F32 = jnp.float32
BF16 = jnp.bfloat16

FAR, IN_UP, IN_DN, NEAR_UP, NEAR_DN, SUM_UP, SUM_DN, SUM_OWN = range(8)
GO_UP1, GO_DN1, GO_UP2, GO_DN2, FWD_UP, FWD_DN, FWD_FAR = range(8, 15)
PER_RUN = 15


def runs_of(n_hid):
    half = (n_hid // 2 + 255) // 256 * 256 if n_hid > 256 else 128
    return ((0, half), (half, n_hid - half))


def relay(
    sizes,
    weights,
    fwd_resid,
    fwd_hidden,
    bwd_resid,
    bwd_hidden,
    saved_pre,
    pool_embed,
    pool_mask,
    pool_stratum,
    order,
    mask_vec,
    ratio_table,
    cot_inject,
    out_resid,
    out_hidden,
    w,
    op,
    res0,
    hin,
    saved0,
    saved,
    embed,
    cot,
    mask_in,
    stratum_in,
    order_in,
    vec_in,
    table_in,
    part,
    far,
    inner,
    near,
    summed,
    total,
    down,
    blend,
    mate_in,
    pair,
    blend_in,
    res_in,
    upd,
    lsem,
    ssem,
    rsem,
):
    n_pipe, n_row, n_col = sizes
    p, r, c = lax.axis_index("pipe"), lax.axis_index("row"), lax.axis_index("col")
    odd = lax.rem(p, 2)
    even = odd == 0
    c_odd = lax.rem(c, 2)
    tc, tr = far.shape[1], res_in.shape[1]
    tokens = tc * n_col
    n_hid, n_feat = w.shape[1], w.shape[0]
    runs = runs_of(n_hid)
    whole = range(len(runs))
    lanes = [pl.ds(at, width) for at, width in runs]
    RES = PER_RUN * len(runs)
    MATE, SPLIT = RES + 1, RES + 3
    SPREAD = SPLIT + n_row // 2
    core, chip, n_chip = lax.rem(r, 2), r // 2, n_row // 2

    def col_at(step):
        return lax.rem(c + (step + n_col), n_col)

    def chip_at(step):
        return lax.rem(chip + step, n_chip)

    def pipe_at(step):
        return lax.rem(p + step + n_pipe, n_pipe)

    partner = p + 1 - 2 * odd
    facing = pipe_at(2 * odd - 1)
    onward = pipe_at(2 - 4 * odd)
    col_far = lax.rem(c + 2 + n_col - 4 * c_odd, n_col)

    barrier = pltpu.get_barrier_semaphore()
    greeted = [{"col": col_at(s)} for s in (1, -1, 2, -2)]
    greeted += [{"pipe": partner, "col": col_at(s)} for s in (0, 2, -2)]
    greeted += [{"pipe": pipe_at(s)} for s in (2, -2)]
    greeted += [{"pipe": facing, "row": 2 * chip_at(s) + core} for s in range(n_chip)]
    greeted += [{"row": lax.rem(r + s, n_row)} for s in range(1, n_row)]
    for device in greeted:
        pl.semaphore_signal(barrier, inc=1, device_id=device, device_id_type=MESH)

    def load(slot, src, dst):
        return pltpu.make_async_copy(src, dst, lsem.at[slot])

    row_tile = pl.ds(pl.multiple_of(r * tr, tr), tr)
    col_tile = pl.ds(pl.multiple_of(c * tc, tc), tc)
    get_w = load(0, weights.at[0], w)
    get_op = load(1, fwd_resid.at[0], op.at[0])
    get_op_odd = load(1, bwd_resid.at[0], op.at[0])
    get_res = load(2, bwd_resid.at[0, row_tile], res0)
    get_res_odd = load(2, fwd_resid.at[0, row_tile], res0)
    get_hin = load(3, bwd_hidden.at[0], hin.at[0])
    get_hin_odd = load(3, fwd_hidden.at[0], hin.at[0])
    get_saved0 = load(4, saved_pre.at[0, 0], saved0)
    get_saved = load(5, saved_pre.at[pl.ds(1, STEPS - 1), 0, col_tile], saved)

    get_w.start()

    @pl.when(even)
    def _():
        get_op.start()
        get_hin.start()
        get_saved0.start()
        get_res.start()

    @pl.when(odd == 1)
    def _():
        get_op_odd.start()
        get_hin_odd.start()
        get_res_odd.start()

    get_saved.start()
    small = [
        load(6, pool_embed.at[:, row_tile], embed),
        load(7, cot_inject.at[:, row_tile], cot),
        load(8, pool_mask, mask_in),
        load(9, pool_stratum, stratum_in),
        load(10, order, order_in),
        load(11, mask_vec, vec_in),
        load(12, ratio_table, table_in),
    ]
    for copy in small:
        copy.start()

    started = []

    def send(k, number, src, dst, device):
        copy = pltpu.make_async_remote_copy(
            src_ref=src,
            dst_ref=dst,
            send_sem=ssem.at[k, number],
            recv_sem=rsem.at[k, number],
            device_id=device,
            device_id_type=MESH,
        )
        copy.start()
        started.append(copy)
        return copy

    def col_view(x):
        return x.reshape(n_col, tc, x.shape[-1])

    def multiply_up(k, h):
        start, width = runs[h]
        for at in range(start, start + width, 256):
            cols = pl.ds(at, min(256, start + width - at))
            out = jnp.dot(op[k], w[:, cols], preferred_element_type=F32)
            part[k, :, :, cols] = col_view(out.astype(BF16))

    def multiply_down(k, h, cols):
        out = lax.dot_general(
            hin[k, :, lanes[h]],
            w[cols, lanes[h]],
            (((1,), (1,)), ((), ())),
            preferred_element_type=F32,
        )
        if h > 0:
            out = out + down[:, cols]
        if h < len(runs) - 1:
            down[:, cols] = out
        else:
            out = out.reshape(n_chip, 2, tr, out.shape[1])
            blend[k, :, :, :, cols] = out.astype(BF16)

    def hin_tile(k, t, h):
        return hin.at[k, pl.ds(pl.multiple_of(t * tc, tc), tc), lanes[h]]

    def share(k, h, number, step, dst, to):
        src = part.at[k, col_at(step), :, lanes[h]]
        return send(k, PER_RUN * h + number, src, dst, {"col": to})

    def sum_start(k, h):
        return (
            share(k, h, FAR, 4, far.at[k, :, lanes[h]], col_far),
            share(k, h, IN_UP, 3, inner.at[k, 0, :, lanes[h]], col_at(1)),
            share(k, h, IN_DN, -3, inner.at[k, 1, :, lanes[h]], col_at(-1)),
        )

    def sum_near(k, h):
        return (
            share(k, h, NEAR_UP, 1, near.at[k, 0, :, lanes[h]], col_at(1)),
            share(k, h, NEAR_DN, -1, near.at[k, 1, :, lanes[h]], col_at(-1)),
        )

    def sum_send(k, h, number, slot, value, step):
        summed[k, slot, :, lanes[h]] = value.astype(BF16)
        src, dst = summed.at[k, slot, :, lanes[h]], total.at[k, slot, :, lanes[h]]
        device = {"col": col_at(step)}
        if k < STEPS - 1:
            device["pipe"] = partner
        return send(k, PER_RUN * h + number, src, dst, device)

    def sum_middle(k, h, arriving):
        ready(arriving)
        run = lanes[h]
        from_far = far[k, :, run].astype(F32)
        up = part[k, col_at(2), :, run].astype(F32) + inner[k, 0, :, run].astype(F32)
        up = up + jnp.where(c_odd == 0, from_far, 0.0)
        a = sum_send(k, h, SUM_UP, 0, up, 2)
        low = part[k, col_at(-2), :, run].astype(F32) + inner[k, 1, :, run].astype(F32)
        low = low + jnp.where(c_odd == 0, 0.0, from_far)
        b = sum_send(k, h, SUM_DN, 1, low, -2)
        return a, b

    def sum_own(k, h, arriving):
        ready(arriving)
        run = lanes[h]
        own = part[k, c, :, run].astype(F32) + near[k, 0, :, run].astype(F32)
        own = own + near[k, 1, :, run].astype(F32)
        if k < STEPS - 1:
            return (sum_send(k, h, SUM_OWN, 2, own, 0),)
        summed[k, 2, :, run] = own.astype(BF16)
        return ()

    def silu(v):
        return v / (1.0 + jnp.exp(-v))

    def sum_end(k, h, arriving):
        ready(arriving)
        run = lanes[h]
        own = summed if k == STEPS - 1 else total
        pre = own[k, 2, :, run].astype(F32)
        pre = pre + total[k, 0, :, run].astype(F32) + total[k, 1, :, run].astype(F32)
        from_even = even if k == STEPS - 1 else odd == 1
        return jnp.where(from_even, silu(pre), pre).astype(BF16)

    def slope(a):
        s = 1.0 / (1.0 + jnp.exp(-a))
        return s * (1.0 + a * (1.0 - s))

    def pass_on(k, h, number, tile, to):
        return send(k, PER_RUN * h + number, tile, tile, {"col": to})

    def go_far(k, h, arriving):
        value = sum_end(k, h, arriving).astype(F32)
        gate = jnp.where(even, slope(saved[k, :, lanes[h]].astype(F32)), 1.0)
        mine = hin_tile(k + 1, c, h)
        mine[...] = (value * gate).astype(BF16)
        return (
            pass_on(k, h, GO_UP2, mine, col_at(2)),
            pass_on(k, h, GO_DN2, mine, col_at(-2)),
        )

    def go_near(k, h):
        mine = hin_tile(k + 1, c, h)
        return (
            pass_on(k, h, GO_UP1, mine, col_at(1)),
            pass_on(k, h, GO_DN1, mine, col_at(-1)),
        )

    def forward(k, h, arriving):
        ready(arriving)
        below = hin_tile(k + 1, col_at(-2), h)
        above = hin_tile(k + 1, col_at(2), h)
        far_tile = hin_tile(k + 1, lax.rem(c + n_col - 2 + 4 * c_odd, n_col), h)
        return (
            pass_on(k, h, FWD_FAR, far_tile, col_far),
            pass_on(k, h, FWD_UP, below, col_at(1)),
            pass_on(k, h, FWD_DN, above, col_at(-1)),
        )

    def chip_steps(last):
        if n_chip != 4:
            return list(range(1 if last else 0, n_chip))
        return [2, 1, 3] if last else [2, 1 + 2 * odd, 0, 3 - 2 * odd]

    def mate_start(k):
        copies = []
        for n in range(2):
            cols = pl.ds(n * (n_feat // 2), n_feat // 2)
            multiply_down(k, len(runs) - 1, cols)
            src, dst = blend.at[k, :, 1 - core, :, cols], mate_in.at[k, :, :, cols]
            copies.append(send(k, MATE + n, src, dst, {"row": r + 1 - 2 * core}))
        return copies

    def blend_start(k, arriving):
        last = k == STEPS - 1
        ready(arriving)
        both = blend[k, :, core].astype(F32) + mate_in[k].astype(F32)
        pair[k] = both.astype(BF16)
        copies = []
        for i, s in enumerate(chip_steps(last)):
            to = chip_at(s)
            device = {"row": 2 * to + core}
            if not last:
                device["pipe"] = facing
            copies.append(send(k, SPLIT + i, pair.at[k, to], blend_in.at[k, i], device))
        return copies

    def blend_end(k, arriving):
        last = k == STEPS - 1
        ready(arriving)
        new = res_in[k].astype(F32)
        if last:
            new = new + pair[k, chip].astype(F32)
        for i in range(len(chip_steps(last))):
            new = new + blend_in[k, i].astype(F32)
        if not last:
            new = jnp.where(p == 0, injected(k), new)
            new = jnp.where(p == n_pipe - 1, cot[k].astype(F32), new)
        dst = upd if last else op.at[k + 1]
        mine = dst.at[row_tile]
        mine[...] = new.astype(BF16)
        copies = []
        for s in [2, 1, 3, 0] if n_chip == 4 else range(n_chip):
            for other in (0, 1) if s else (1,):
                to = 2 * chip_at(s) + core + other * (1 - 2 * core)
                copies.append(send(k, SPREAD + 2 * s + other, mine, mine, {"row": to}))
        return copies

    def pick(index, ref):
        value = ref[ref.shape[0] - 1]
        for i in range(ref.shape[0] - 1):
            value = jnp.where(index == i, ref[i], value)
        return value

    def injected(k):
        chosen = order_in[k]
        stratum = pick(chosen, stratum_in)
        mask = mask_in[pl.ds(mask_in.shape[0] - 1, 1), :]
        for i in range(mask_in.shape[0] - 1):
            mask = jnp.where(chosen == i, mask_in[pl.ds(i, 1), :], mask)
        here = lax.broadcasted_iota(jnp.int32, (tr, tokens), 0) + r * tr
        there = lax.broadcasted_iota(jnp.int32, (tr, tokens), 1)
        column = jnp.where(here == there, jnp.broadcast_to(mask, (tr, tokens)), 0)
        masked = jnp.sum(column.astype(F32), axis=1, keepdims=True) == 1.0
        table = table_in[...].astype(F32)
        strata = lax.broadcasted_iota(jnp.int32, table.shape, 0)
        condition = jnp.sum(jnp.where(strata == stratum, table, 0.0), axis=0, keepdims=True)
        vec = jnp.broadcast_to(vec_in[...].astype(F32)[None], (tr, n_feat))
        rows = jnp.where(masked, vec, pick(chosen, embed).astype(F32))
        return rows + condition

    def ready(copies):
        for copy in copies:
            copy.wait_recv()

    def starts(k):
        return [sum_start(k, h) for h in whole]

    def nears(k):
        return [sum_near(k, h) for h in whole]

    def ups(k):
        for h in whole:
            multiply_up(k, h)

    def middles(k, arriving, beside):
        sums = [sum_middle(k, h, arriving[h]) for h in whole]
        return [sums[h] + sum_own(k, h, beside[h]) for h in whole]

    def gathers(k, arriving):
        return [go_far(k, h, arriving[h]) for h in whole]

    def goes(k):
        return [go_near(k, h) for h in whole]

    def forwards(k, arriving):
        return [forward(k, h, arriving[h]) for h in whole]

    def mates(k, arriving, beside):
        for h in whole:
            ready(arriving[h] + beside[h])
            if h < len(runs) - 1:
                for n in range(2):
                    multiply_down(k, h, pl.ds(n * (n_feat // 2), n_feat // 2))
        return mate_start(k)

    def send_res(k):
        to = partner if k == STEPS - 2 else onward
        return [send(k + 1, RES, op.at[k, row_tile], res_in.at[k + 1], {"pipe": to})]

    nothing = [(), ()]
    get_op.wait()
    get_w.wait()
    ups(0)
    pl.semaphore_wait(barrier, len(greeted))
    x = starts(0)
    xn = nears(0)
    get_hin.wait()

    @pl.when(even)
    def _():
        get_saved0.wait()
        hin[0] = (hin[0].astype(F32) * slope(saved0[...].astype(F32))).astype(BF16)

    y = mates(0, nothing, nothing)
    get_res.wait()
    y_res = [send(0, RES, res0, res_in.at[0], {"pipe": facing})]
    y = blend_start(0, y)
    x_res = send_res(0)
    get_saved.wait()
    for copy in small:
        copy.wait()
    x = middles(0, x, xn)
    x = gathers(0, x)
    xn = goes(0)
    y = blend_end(0, y + y_res)
    x = forwards(0, x)
    ready(y)
    ups(1)
    y = starts(1)
    yn = nears(1)
    y_res = send_res(1)
    x = mates(1, x, xn)
    x = blend_start(1, x)
    y = middles(1, y, yn)
    x = blend_end(1, x + x_res)
    y = gathers(1, y)
    yn = goes(1)
    ready(x)
    ups(2)
    x = starts(2)
    y = forwards(1, y)
    xn = nears(2)
    x_res = send_res(2)
    x = middles(2, x, xn)
    y = mates(2, y, yn)
    y = blend_start(2, y)
    x = gathers(2, x)
    xn = goes(2)
    y = blend_end(2, y + y_res)
    x = forwards(2, x)
    ready(y)
    ups(3)
    y = starts(3)
    yn = nears(3)
    out_resid[odd, 0] = op[3]
    x = mates(3, x, xn)
    x = blend_start(3, x)
    y = middles(3, y, yn)
    for h in whole:
        out_hidden[0, :, lanes[h]] = sum_end(3, h, y[h])
    x = blend_end(3, x + x_res)
    ready(x)
    out_resid[1 - odd, 0] = upd[...]
    for copy in started:
        copy.wait_send()


def solution(mesh):
    sizes = tuple(mesh.shape[a] for a in ("pipe", "row", "col"))
    n_pipe, n_row, n_col = sizes

    def shards(weights, fwd_resid, fwd_hidden, *rest):
        _, tokens, n_feat = fwd_resid.shape
        n_hid = fwd_hidden.shape[2]
        tc, tr = tokens // n_col, tokens // n_row
        pool = rest[3].shape[0]
        hbm = pl.BlockSpec(memory_space=pltpu.HBM)
        vmem = pl.BlockSpec(memory_space=pltpu.VMEM)
        n_chip = n_row // 2
        copies = PER_RUN * len(runs_of(n_hid)) + 3 + n_chip + n_row
        return pl.pallas_call(
            functools.partial(relay, sizes),
            out_shape=(
                jax.ShapeDtypeStruct((2, 1, tokens, n_feat), BF16),
                jax.ShapeDtypeStruct((1, tc, n_hid), BF16),
            ),
            in_specs=[hbm] * 13,
            out_specs=(vmem, vmem),
            scratch_shapes=[
                pltpu.VMEM((n_feat, n_hid), BF16),
                pltpu.VMEM((STEPS, tokens, n_feat), BF16),
                pltpu.VMEM((tr, n_feat), BF16),
                pltpu.VMEM((STEPS, tokens, n_hid), BF16),
                pltpu.VMEM((tokens, n_hid), BF16),
                pltpu.VMEM((STEPS - 1, tc, n_hid), BF16),
                pltpu.VMEM((pool, tr, n_feat), BF16),
                pltpu.VMEM((pool, tr, n_feat), BF16),
                pltpu.VMEM((pool, tokens), jnp.int32),
                pltpu.SMEM((pool,), jnp.int32),
                pltpu.SMEM((pool,), jnp.int32),
                pltpu.VMEM((n_feat,), BF16),
                pltpu.VMEM((rest[8].shape[0], n_feat), BF16),
                pltpu.VMEM((STEPS, n_col, tc, n_hid), BF16),
                pltpu.VMEM((STEPS, tc, n_hid), BF16),
                pltpu.VMEM((STEPS, 2, tc, n_hid), BF16),
                pltpu.VMEM((STEPS, 2, tc, n_hid), BF16),
                pltpu.VMEM((STEPS, 3, tc, n_hid), BF16),
                pltpu.VMEM((STEPS, 3, tc, n_hid), BF16),
                pltpu.VMEM((tokens, n_feat), F32),
                pltpu.VMEM((STEPS, n_chip, 2, tr, n_feat), BF16),
                pltpu.VMEM((STEPS, n_chip, tr, n_feat), BF16),
                pltpu.VMEM((STEPS, n_chip, tr, n_feat), BF16),
                pltpu.VMEM((STEPS, n_chip, tr, n_feat), BF16),
                pltpu.VMEM((STEPS, tr, n_feat), BF16),
                pltpu.VMEM((tokens, n_feat), BF16),
                pltpu.SemaphoreType.DMA((13,)),
                pltpu.SemaphoreType.DMA((STEPS, copies)),
                pltpu.SemaphoreType.DMA((STEPS, copies)),
            ],
            compiler_params=pltpu.CompilerParams(
                collective_id=0, has_side_effects=True, vmem_limit_bytes=60 * 1024 * 1024
            ),
        )(weights, fwd_resid, fwd_hidden, *rest)

    return jax.shard_map(
        shards,
        mesh=mesh,
        in_specs=(
            P("pipe", "col", "row"),
            P("pipe", None, "col"),
            P("pipe", None, "row"),
            P("pipe", None, "col"),
            P("pipe", None, "row"),
            P(None, "pipe", None, "row"),
            P(None, None, "col"),
            P(),
            P(),
            P(),
            P("col"),
            P(None, "col"),
            P(None, None, "col"),
        ),
        out_specs=(P(None, "pipe", None, "col"), P("pipe", "col", "row")),
        check_vma=False,
    )
```

time: 109 us -> 102 us (0.936); the launches traced: 108 us -> 102 us
  Pallas kernels: 104 us -> 98.3 us
    pallas_call x1, Pallas kernels: 104 us -> 98.3 us  [shards(): pl.pallas_call(functools.partial(relay, sizes), out_shape=(jax.ShapeDtype...]
where the time goes in v3:
time: 102 us
  Pallas kernels  98.3 us (96%)
  local copies, waits for them, and re-layouts  3.11 us (3%)
    pallas_call x1, Pallas kernels, shards(): pl.pallas_call(functools.partial(relay, sizes), out_shape=(jax.ShapeDtype...  98.3 us
    unnamed x2, local copies, waits for them, and re-layouts  3.11 us

profile of v3, /device:TPU:1, one launch (start us, length us, event | category | flops | bytes accessed | tf_op | source)
XLA Modules:
  0.0 102.1 jit_solution(15544930836680439352)
XLA Ops:
  0.6 98.3 %shard_map.140 = (bf16[2,1,128,512]{3,2,1,0:T(8,128)(2,1)}, bf16[1,16,1792]{2,1,0:T(8,128)(2,1)}) custom-call(bf16[1,512,1792]{2,1,0:T(8,128)(2,1)} %weights.1, bf16[1,128,512]{2,1,0:T(8,128)(2,1)} %fwd_resid.1, bf16[1,128,1792]{2,1,0:T(8,128)(2,1)} %fwd_hidden.1, bf16[1,128,512]{2,1,0:T(8,128)(2,1)} %bwd_resid.1, bf16[1,128,1792]{2,1,0:T(8,128)(2,1)} %bwd_hidden.1, ...), custom_call_target="tpu_custom_call" | custom-call | tf_op jit(solution)/shard_map/pallas_call | solution.py:483
  99.0 1.7 %copy.17 = bf16[2,1,128,512]{3,2,1,0:T(8,128)(2,1)} copy(bf16[2,1,128,512]{3,2,1,0:T(8,128)(2,1)} %get-tuple-element.4) | data formatting | bytes 524288
  100.6 1.4 %copy.18 = bf16[1,16,1792]{2,1,0:T(8,128)(2,1)} copy(bf16[1,16,1792]{2,1,0:T(8,128)(2,1)} %get-tuple-element.5) | data formatting | bytes 114688

commit v4 on v3

--- a/solution.py
+++ b/solution.py
@@ -99,14 +99,26 @@
     onward = pipe_at(2 - 4 * odd)
     col_far = lax.rem(c + 2 + n_col - 4 * c_odd, n_col)
 
+    inside = (p > 0) & (p < n_pipe - 1)
+    above, below = p < n_pipe - 2, p > 1
+    has_onward = (p != 1) & (p != n_pipe - 2)
+
     barrier = pltpu.get_barrier_semaphore()
     greeted = [{"col": col_at(s)} for s in (1, -1, 2, -2)]
     greeted += [{"pipe": partner, "col": col_at(s)} for s in (0, 2, -2)]
-    greeted += [{"pipe": pipe_at(s)} for s in (2, -2)]
-    greeted += [{"pipe": facing, "row": 2 * chip_at(s) + core} for s in range(n_chip)]
     greeted += [{"row": lax.rem(r + s, n_row)} for s in range(1, n_row)]
-    for device in greeted:
-        pl.semaphore_signal(barrier, inc=1, device_id=device, device_id_type=MESH)
+    across = [{"pipe": facing, "row": 2 * chip_at(s) + core} for s in range(n_chip)]
+
+    def greet(devices):
+        for device in devices:
+            pl.semaphore_signal(barrier, inc=1, device_id=device, device_id_type=MESH)
+
+    pl.when(inside)(lambda: greet(across))
+    pl.when(above)(lambda: greet([{"pipe": pipe_at(2)}]))
+    pl.when(below)(lambda: greet([{"pipe": pipe_at(-2)}]))
+    greet(greeted)
+    greetings = len(greeted) + jnp.where(inside, n_chip, 0)
+    greetings = greetings + jnp.where(above, 1, 0) + jnp.where(below, 1, 0)
 
     def load(slot, src, dst):
         return pltpu.make_async_copy(src, dst, lsem.at[slot])
@@ -153,7 +165,7 @@
 
     started = []
 
-    def send(k, number, src, dst, device):
+    def send(k, number, src, dst, device, when=None):
         copy = pltpu.make_async_remote_copy(
             src_ref=src,
             dst_ref=dst,
@@ -162,8 +174,11 @@
             device_id=device,
             device_id_type=MESH,
         )
-        copy.start()
-        started.append(copy)
+        if when is None:
+            copy.start()
+        else:
+            pl.when(when)(copy.start)
+        started.append((copy, when))
         return copy
 
     def col_view(x):
@@ -313,23 +328,36 @@
             device = {"row": 2 * to + core}
             if not last:
                 device["pipe"] = facing
-            copies.append(send(k, SPLIT + i, pair.at[k, to], blend_in.at[k, i], device))
+            src, dst = pair.at[k, to], blend_in.at[k, i]
+            copies.append(send(k, SPLIT + i, src, dst, device, None if last else inside))
         return copies
 
     def blend_end(k, arriving):
         last = k == STEPS - 1
-        ready(arriving)
-        new = res_in[k].astype(F32)
+        mine = (upd if last else op.at[k + 1]).at[row_tile]
+
+        def finish():
+            ready(arriving)
+            new = res_in[k].astype(F32)
+            if last:
+                new = new + pair[k, chip].astype(F32)
+            for i in range(len(chip_steps(last))):
+                new = new + blend_in[k, i].astype(F32)
+            mine[...] = new.astype(BF16)
+
         if last:
-            new = new + pair[k, chip].astype(F32)
-        for i in range(len(chip_steps(last))):
-            new = new + blend_in[k, i].astype(F32)
-        if not last:
-            new = jnp.where(p == 0, injected(k), new)
-            new = jnp.where(p == n_pipe - 1, cot[k].astype(F32), new)
-        dst = upd if last else op.at[k + 1]
-        mine = dst.at[row_tile]
-        mine[...] = new.astype(BF16)
+            finish()
+        else:
+            pl.when(inside)(finish)
+
+            @pl.when(p == 0)
+            def _():
+                mine[...] = injected(k).astype(BF16)
+
+            @pl.when(p == n_pipe - 1)
+            def _():
+                mine[...] = cot[k]
+
         copies = []
         for s in [2, 1, 3, 0] if n_chip == 4 else range(n_chip):
             for other in (0, 1) if s else (1,):
@@ -396,14 +424,16 @@
         return mate_start(k)
 
     def send_res(k):
-        to = partner if k == STEPS - 2 else onward
-        return [send(k + 1, RES, op.at[k, row_tile], res_in.at[k + 1], {"pipe": to})]
+        src, dst = op.at[k, row_tile], res_in.at[k + 1]
+        if k == STEPS - 2:
+            return [send(k + 1, RES, src, dst, {"pipe": partner})]
+        return [send(k + 1, RES, src, dst, {"pipe": onward}, has_onward)]
 
     nothing = [(), ()]
     get_op.wait()
     get_w.wait()
     ups(0)
-    pl.semaphore_wait(barrier, len(greeted))
+    pl.semaphore_wait(barrier, greetings)
     x = starts(0)
     xn = nears(0)
     get_hin.wait()
@@ -415,7 +445,7 @@
 
     y = mates(0, nothing, nothing)
     get_res.wait()
-    y_res = [send(0, RES, res0, res_in.at[0], {"pipe": facing})]
+    y_res = [send(0, RES, res0, res_in.at[0], {"pipe": facing}, inside)]
     y = blend_start(0, y)
     x_res = send_res(0)
     get_saved.wait()
@@ -440,8 +470,8 @@
     ready(x)
     ups(2)
     x = starts(2)
+    xn = nears(2)
     y = forwards(1, y)
-    xn = nears(2)
     x_res = send_res(2)
     x = middles(2, x, xn)
     y = mates(2, y, yn)
@@ -463,8 +493,11 @@
     x = blend_end(3, x + x_res)
     ready(x)
     out_resid[1 - odd, 0] = upd[...]
-    for copy in started:
-        copy.wait_send()
+    for copy, when in started:
+        if when is None:
+            copy.wait_send()
+        else:
+            pl.when(when)(copy.wait_send)
 
 
 def solution(mesh):

time: 102 us -> 94.6 us (0.927)
  the two profiles are of different devices: /device:TPU:1 before, /device:TPU:259 now
where the time goes in v4:
time: 94.6 us; the launch traced here: 94.4 us
  Pallas kernels  90.7 us (96%)
  local copies, waits for them, and re-layouts  3.11 us (3%)
    pallas_call x1, Pallas kernels, shards(): pl.pallas_call(functools.partial(relay, sizes), out_shape=(jax.ShapeDtype...  90.7 us
    unnamed x2, local copies, waits for them, and re-layouts  3.11 us

profile of v4, /device:TPU:259, one launch (start us, length us, event | category | flops | bytes accessed | tf_op | source)
XLA Modules:
  0.0 94.4 jit_solution(11235878502609882090)
XLA Ops:
  0.6 90.7 %shard_map.140 = (bf16[2,1,128,512]{3,2,1,0:T(8,128)(2,1)}, bf16[1,16,1792]{2,1,0:T(8,128)(2,1)}) custom-call(bf16[1,512,1792]{2,1,0:T(8,128)(2,1)} %weights.1, bf16[1,128,512]{2,1,0:T(8,128)(2,1)} %fwd_resid.1, bf16[1,128,1792]{2,1,0:T(8,128)(2,1)} %fwd_hidden.1, bf16[1,128,512]{2,1,0:T(8,128)(2,1)} %bwd_resid.1, bf16[1,128,1792]{2,1,0:T(8,128)(2,1)} %bwd_hidden.1, ...), custom_call_target="tpu_custom_call" | custom-call | tf_op jit(solution)/shard_map/pallas_call | solution.py:516
  91.3 1.7 %copy.17 = bf16[2,1,128,512]{3,2,1,0:T(8,128)(2,1)} copy(bf16[2,1,128,512]{3,2,1,0:T(8,128)(2,1)} %get-tuple-element.4) | data formatting | bytes 524288
  93.0 1.4 %copy.18 = bf16[1,16,1792]{2,1,0:T(8,128)(2,1)} copy(bf16[1,16,1792]{2,1,0:T(8,128)(2,1)} %get-tuple-element.5) | data formatting | bytes 114688

commit v5 on v4

--- a/solution.py
+++ b/solution.py
@@ -65,6 +65,7 @@
     blend_in,
     res_in,
     upd,
+    hid,
     lsem,
     ssem,
     rsem,
@@ -135,6 +136,10 @@
     get_saved0 = load(4, saved_pre.at[0, 0], saved0)
     get_saved = load(5, saved_pre.at[pl.ds(1, STEPS - 1), 0, col_tile], saved)
 
+    put_op = load(13, op.at[STEPS - 1], out_resid.at[odd, 0])
+    put_upd = load(14, upd, out_resid.at[1 - odd, 0])
+    put_hid = load(15, hid, out_hidden.at[0])
+
     get_w.start()
 
     @pl.when(even)
@@ -402,8 +407,10 @@
         for h in whole:
             multiply_up(k, h)
 
-    def middles(k, arriving, beside):
-        sums = [sum_middle(k, h, arriving[h]) for h in whole]
+    def middles(k, arriving):
+        return [sum_middle(k, h, arriving[h]) for h in whole]
+
+    def owns(k, sums, beside):
         return [sums[h] + sum_own(k, h, beside[h]) for h in whole]
 
     def gathers(k, arriving):
@@ -451,7 +458,8 @@
     get_saved.wait()
     for copy in small:
         copy.wait()
-    x = middles(0, x, xn)
+    x = middles(0, x)
+    x = owns(0, x, xn)
     x = gathers(0, x)
     xn = goes(0)
     y = blend_end(0, y + y_res)
@@ -463,41 +471,62 @@
     y_res = send_res(1)
     x = mates(1, x, xn)
     x = blend_start(1, x)
-    y = middles(1, y, yn)
+    y = middles(1, y)
+    y = owns(1, y, yn)
     x = blend_end(1, x + x_res)
     y = gathers(1, y)
     yn = goes(1)
     ready(x)
     ups(2)
     x = starts(2)
+    y = forwards(1, y)
     xn = nears(2)
-    y = forwards(1, y)
     x_res = send_res(2)
-    x = middles(2, x, xn)
+    x = middles(2, x)
     y = mates(2, y, yn)
     y = blend_start(2, y)
+    x = owns(2, x, xn)
     x = gathers(2, x)
     xn = goes(2)
+    x = forwards(2, x)
     y = blend_end(2, y + y_res)
-    x = forwards(2, x)
+    x = mates(3, x, xn)
+    x = blend_start(3, x)
     ready(y)
+    put_op.start()
     ups(3)
     y = starts(3)
     yn = nears(3)
-    out_resid[odd, 0] = op[3]
-    x = mates(3, x, xn)
-    x = blend_start(3, x)
-    y = middles(3, y, yn)
+    y = middles(3, y)
+    y = owns(3, y, yn)
+    x = blend_end(3, x + x_res)
     for h in whole:
-        out_hidden[0, :, lanes[h]] = sum_end(3, h, y[h])
-    x = blend_end(3, x + x_res)
+        hid[:, lanes[h]] = sum_end(3, h, y[h])
+    put_hid.start()
     ready(x)
-    out_resid[1 - odd, 0] = upd[...]
+    put_upd.start()
     for copy, when in started:
         if when is None:
             copy.wait_send()
         else:
             pl.when(when)(copy.wait_send)
+    for copy in (put_op, put_upd, put_hid):
+        copy.wait()
+
+
+def hand_out(res, hid, out_res, out_hid, res_here, hid_here, sem):
+    half = res.shape[0] // 2
+    parts = [(res.at[pl.ds(i * half, half)], res_here.at[i], out_res.at[pl.ds(i * half, half)]) for i in range(2)]
+    parts.append((hid, hid_here, out_hid))
+    get = [pltpu.make_async_copy(a, b, sem.at[i]) for i, (a, b, _) in enumerate(parts)]
+    put = [pltpu.make_async_copy(b, c, sem.at[3 + i]) for i, (_, b, c) in enumerate(parts)]
+    for copy in get:
+        copy.start()
+    for first, second in zip(get, put):
+        first.wait()
+        second.start()
+    for copy in put:
+        copy.wait()
 
 
 def solution(mesh):
@@ -510,17 +539,16 @@
         tc, tr = tokens // n_col, tokens // n_row
         pool = rest[3].shape[0]
         hbm = pl.BlockSpec(memory_space=pltpu.HBM)
-        vmem = pl.BlockSpec(memory_space=pltpu.VMEM)
         n_chip = n_row // 2
         copies = PER_RUN * len(runs_of(n_hid)) + 3 + n_chip + n_row
-        return pl.pallas_call(
+        out, hid_out = pl.pallas_call(
             functools.partial(relay, sizes),
             out_shape=(
                 jax.ShapeDtypeStruct((2, 1, tokens, n_feat), BF16),
                 jax.ShapeDtypeStruct((1, tc, n_hid), BF16),
             ),
             in_specs=[hbm] * 13,
-            out_specs=(vmem, vmem),
+            out_specs=(hbm, hbm),
             scratch_shapes=[
                 pltpu.VMEM((n_feat, n_hid), BF16),
                 pltpu.VMEM((STEPS, tokens, n_feat), BF16),
@@ -548,7 +576,8 @@
                 pltpu.VMEM((STEPS, n_chip, tr, n_feat), BF16),
                 pltpu.VMEM((STEPS, tr, n_feat), BF16),
                 pltpu.VMEM((tokens, n_feat), BF16),
-                pltpu.SemaphoreType.DMA((13,)),
+                pltpu.VMEM((tc, n_hid), BF16),
+                pltpu.SemaphoreType.DMA((16,)),
                 pltpu.SemaphoreType.DMA((STEPS, copies)),
                 pltpu.SemaphoreType.DMA((STEPS, copies)),
             ],
@@ -556,6 +585,21 @@
                 collective_id=0, has_side_effects=True, vmem_limit_bytes=60 * 1024 * 1024
             ),
         )(weights, fwd_resid, fwd_hidden, *rest)
+        return pl.pallas_call(
+            hand_out,
+            out_shape=(
+                jax.ShapeDtypeStruct(out.shape, BF16),
+                jax.ShapeDtypeStruct(hid_out.shape, BF16),
+            ),
+            in_specs=[hbm] * 2,
+            out_specs=(hbm, hbm),
+            scratch_shapes=[
+                pltpu.VMEM((2, 1, 1, tokens, n_feat), BF16),
+                pltpu.VMEM(hid_out.shape, BF16),
+                pltpu.SemaphoreType.DMA((6,)),
+            ],
+            compiler_params=pltpu.CompilerParams(vmem_limit_bytes=60 * 1024 * 1024),
+        )(out, hid_out)
 
     return jax.shard_map(
         shards,

time: 94.6 us -> 92.9 us (0.982)
  the two profiles are of different devices: /device:TPU:259 before, /device:TPU:1 now
where the time goes in v5:
time: 92.9 us; the launch traced here: 92.7 us
  Pallas kernels  92.1 us (99%)
    pallas_call x1, Pallas kernels, shards(): pl.pallas_call(functools.partial(relay, sizes), out_shape=(jax.ShapeDtype...  90.4 us

profile of v5, /device:TPU:1, one launch (start us, length us, event | category | flops | bytes accessed | tf_op | source)
XLA Modules:
  0.0 92.7 jit_solution(3308072584765935843)
XLA Ops:
  0.6 90.4 %shard_map.140 = (bf16[2,1,128,512]{3,2,1,0:T(8,128)(2,1)}, bf16[1,16,1792]{2,1,0:T(8,128)(2,1)}) custom-call(bf16[1,512,1792]{2,1,0:T(8,128)(2,1)} %weights.1, bf16[1,128,512]{2,1,0:T(8,128)(2,1)} %fwd_resid.1, bf16[1,128,1792]{2,1,0:T(8,128)(2,1)} %fwd_hidden.1, bf16[1,128,512]{2,1,0:T(8,128)(2,1)} %bwd_resid.1, bf16[1,128,1792]{2,1,0:T(8,128)(2,1)} %bwd_hidden.1, ...), custom_call_target="tpu_custom_call" | custom-call | tf_op jit(solution)/shard_map/pallas_call | solution.py:544
  91.0 1.7 %shard_map.141 = (bf16[2,1,128,512]{3,2,1,0:T(8,128)(2,1)}, bf16[1,16,1792]{2,1,0:T(8,128)(2,1)}) custom-call(bf16[2,1,128,512]{3,2,1,0:T(8,128)(2,1)} %get-tuple-element.4.res, bf16[1,16,1792]{2,1,0:T(8,128)(2,1)} %get-tuple-element.5.hid), custom_call_target="tpu_custom_call" | custom-call | tf_op jit(solution)/shard_map/pallas_call | solution.py:588
